TPU v7x, 32 devices: a whole 2x2x4 slice. The times are simulated.
32 devices in a mesh: blk: 16 (over z, y, x), grp: 2 (over core).
Axes of the slice: x: 2, y: 2, z: 4, core: 2. Of those that a mesh axis runs over, the one named last changes fastest.
Arguments:
- points: bfloat16 [64, 4096], P(None, ('blk', 'grp')), may hold values from -6 to 6
- right_side: float32 [16, 4096], P(None, ('blk', 'grp')), may hold values from -18 to 18
- lengthscale: float32 [1], replicated, may hold values from 3.3110573 to 4.0550324
- outputscale: float32 [1], replicated, may hold values from 0.6 to 1.6
- noise_level: float32 [1], replicated, may hold values from 0.4 to 1
Outputs:
- solution: float32 [16, 4096], P(None, ('blk', 'grp'))
- residual: float32 [16, 4096], P(None, ('blk', 'grp'))
- gradient: float32 [3], replicated
All inputs are finite; a program needn't handle non-finite values.
Results may differ from a plain program's by a relative error of at most 0.001.
The roundings to bfloat16 on the way count: a program that leaves them out, or rounds other values in their place, can miss the bound.
Values may be sent and summed in bfloat16 or wider, within the bound.
No kernel may reach another device: no remote copies, remote signals or barrier semaphores. Data moves between devices by JAX's collectives and lax.ppermute only.
A program may use at most 64 MiB of HBM per device.

v0:
```python
import math

import jax
import jax.numpy as jnp
from jax import lax
from jax.sharding import PartitionSpec as P

ITERS = 2


def kernel_tiles(own_points, own_squares, tile_points, scale_len, with_grad):
    tile_squares = jnp.sum(jnp.square(tile_points.astype(jnp.float32)), axis=0)
    inner_prod = lax.dot_general(
        own_points, tile_points, (((0,), (0,)), ((), ())), preferred_element_type=jnp.float32
    )
    distance = jnp.maximum(own_squares[:, None] + tile_squares[None, :] - 2.0 * inner_prod, 0.0)
    radius = jnp.sqrt(5.0 * distance) / scale_len
    damping = jnp.exp(-radius)
    tiles = [((1.0 + radius + radius * radius / 3.0) * damping).astype(jnp.bfloat16)]
    if with_grad:
        tiles.append(
            (radius * radius * (1.0 + radius) * damping / (3.0 * scale_len)).astype(jnp.bfloat16)
        )
    return tiles


def apply_columns(tile_vectors, single):
    return lax.dot_general(
        tile_vectors, single, (((1,), (1,)), ((), ())), preferred_element_type=jnp.float32
    )


def sweep(own_side, visitor, scale_len, with_grad, forward_sum, backward_sum):
    own_points, own_squares, own_vectors = own_side
    visit_points, visit_vectors = visitor
    column_count = visit_points.shape[1]
    block_width = math.gcd(column_count, max(512, own_points.shape[1]))

    def one_block(block_index, carried):
        forward_sum, backward_sum = carried
        offset = block_index * block_width
        tile_points = lax.dynamic_slice_in_dim(visit_points, offset, block_width, 1)
        tile_vectors = lax.dynamic_slice_in_dim(visit_vectors, offset, block_width, 1)
        tiles = kernel_tiles(own_points, own_squares, tile_points, scale_len, with_grad)
        forward_sum = forward_sum + jnp.concatenate(
            [apply_columns(tile_vectors, single) for single in tiles], axis=0
        )
        return (forward_sum, backward_sum)

    return lax.fori_loop(0, column_count // block_width, one_block, (forward_sum, backward_sum))


def local(points, right_side, lengthscale, outputscale, noise_level):
    scale_len = lengthscale[0]
    amplitude = outputscale[0]
    jitter = noise_level[0]
    squares = jnp.sum(jnp.square(points.astype(jnp.float32)), axis=0)
    column_count = right_side.shape[0]
    own_rows = points.shape[1]

    def kernel_product(vectors, with_grad):
        rounded = vectors.astype(jnp.bfloat16)
        own_side = (points, squares, rounded)
        out_rows = column_count * (2 if with_grad else 1)
        empty = jnp.zeros((out_rows, own_rows), jnp.float32)
        forward_sum, unused = sweep(
            own_side,
            (
                lax.all_gather(points, ("blk", "grp"), axis=1, tiled=True),
                lax.all_gather(rounded, ("blk", "grp"), axis=1, tiled=True),
            ),
            scale_len,
            with_grad,
            empty,
            None,
        )
        return forward_sum

    def system(vectors):
        return amplitude * kernel_product(vectors, False) + jitter * vectors

    solution = jnp.zeros_like(right_side)
    residual = right_side
    direction = right_side
    norm_now = lax.psum(jnp.sum(residual * residual, axis=1), ("blk", "grp"))
    applied = system(direction)
    curvature = lax.psum(jnp.sum(direction * applied, axis=1), ("blk", "grp"))
    for iteration in range(ITERS):
        if iteration > 0:
            applied = system(direction)
            curvature = lax.psum(jnp.sum(direction * applied, axis=1), ("blk", "grp"))
        step_size = norm_now / curvature
        solution = solution + step_size[:, None] * direction
        residual = residual - step_size[:, None] * applied
        if iteration + 1 < ITERS:
            norm_next = lax.psum(jnp.sum(residual * residual, axis=1), ("blk", "grp"))
            direction = residual + (norm_next / norm_now)[:, None] * direction
            norm_now = norm_next
    products_out = kernel_product(solution, True)
    kernel_part = products_out[:column_count]
    slope_part = products_out[column_count:]
    left_side = jnp.concatenate([solution[:1], right_side[1:]], axis=0)
    weights = jnp.where(
        lax.iota(jnp.int32, column_count) == 0, 1.0, -1.0 / (column_count - 1)
    ).astype(jnp.float32)[:, None]
    local_terms = jnp.stack(
        [
            jnp.sum(weights * left_side * amplitude * slope_part),
            jnp.sum(weights * left_side * kernel_part),
            jnp.sum(weights * left_side * solution),
        ]
    )
    total_points = own_rows * lax.axis_size("blk") * lax.axis_size("grp")
    gradient = 0.5 * lax.psum(local_terms, ("blk", "grp")) / total_points
    return (solution, residual, gradient)


def solution(mesh):
    in_specs = (P(None, ("blk", "grp")), P(None, ("blk", "grp")), P(), P(), P())
    out_specs = (P(None, ("blk", "grp")), P(None, ("blk", "grp")), P())
    return jax.shard_map(local, mesh=mesh, in_specs=in_specs, out_specs=out_specs, check_vma=False)
```

profile of v0, /device:TPU:0, one launch (start us, length us, event | category | flops | bytes accessed | tf_op | source)
XLA Modules:
  0.0 352.7 jit_solution(17801791447850920432)
XLA Ops:
  0.6 44.9 %all_gather.15 = bf16[64,4096]{1,0:T(8,128)(2,1)S(1)} all-gather(bf16[64,128]{1,0:T(8,128)(2,1)} %param.11), channel_id=1, replica_groups=mesh['blk'=16,'grp'=2] {'blk','grp'}, dimensions={1}, use_global_device_ids=true | all-gather | bytes 540672 | tf_op jit(solution)/shard_map/all_gather | solution.py:69
  45.6 0.7 copy-done
  46.3 37.0 %all_gather.14 = bf16[16,4096]{1,0:T(8,128)(2,1)S(1)} all-gather(bf16[16,128]{1,0:T(8,128)(2,1)S(1)} %convert_element_type.64), channel_id=1, replica_groups=mesh['blk'=16,'grp'=2] {'blk','grp'}, dimensions={1}, use_global_device_ids=true | all-gather | bytes 135168 | tf_op jit(solution)/shard_map/all_gather | solution.py:70
  83.2 9.4 %while.43 = (s32[]{:T(128)}, f32[16,128]{1,0:T(8,128)S(1)}, bf16[16,4096]{1,0:T(8,128)(2,1)S(1)}, f32[128]{0:T(128)S(1)}, bf16[64,4096]{1,0:T(8,128)(2,1)S(1)}, ...) while((s32[]{:T(128)}, f32[16,128]{1,0:T(8,128)S(1)}, ...), condition=%wide.region_5.0_spmd.clone, body=%wide.region_3.0_spmd.clone.sunk | while | flops 11439623 | bytes 186540 | solution.py:50
  83.3 1.1 convolution_add_fusion.4
  84.4 1.1 convolution_add_fusion.4
  85.6 1.1 convolution_add_fusion.4
  86.8 1.1 convolution_add_fusion.4
  88.0 1.1 convolution_add_fusion.4
  89.1 1.1 convolution_add_fusion.4
  90.3 1.1 convolution_add_fusion.4
  91.5 1.1 convolution_add_fusion.4
  94.0 36.9 %all-reduce = (f32[16]{0:T(128)S(1)}, f32[16]{0:T(128)S(1)}) all-reduce(f32[16]{0:T(128)S(1)} %get-tuple-element.490, f32[16]{0:T(128)S(1)} %get-tuple-element.489), channel_id=1, replica_groups=mesh['blk'=16,'grp'=2] {'blk','grp'}, use_global_device_ids=true, to_apply=%region_1.0 | all-reduce | flops 32 | bytes 256 | tf_op jit(solution)/shard_map/psum | solution.py:85
  131.2 42.4 %psum.37 = f32[16]{0:T(128)S(1)} all-reduce(f32[16]{0:T(128)S(1)} %multiply_reduce_fusion.8), channel_id=1, replica_groups=mesh['blk'=16,'grp'=2] {'blk','grp'}, use_global_device_ids=true, to_apply=%region_9.0 | all-reduce | flops 16 | bytes 128 | tf_op jit(solution)/shard_map/psum | solution.py:96
  173.7 39.7 %all_gather.16 = bf16[16,4096]{1,0:T(8,128)(2,1)S(1)} all-gather(bf16[16,128]{1,0:T(8,128)(2,1)S(1)} %fusion.67), channel_id=1, replica_groups=mesh['blk'=16,'grp'=2] {'blk','grp'}, dimensions={1}, use_global_device_ids=true | all-gather | bytes 135168 | tf_op jit(solution)/shard_map/all_gather | solution.py:70
  213.3 9.4 %while.44 = (s32[]{:T(128)}, f32[16,128]{1,0:T(8,128)S(1)}, bf16[16,4096]{1,0:T(8,128)(2,1)S(1)}, f32[128]{0:T(128)S(1)}, bf16[64,4096]{1,0:T(8,128)(2,1)S(1)}, ...) while((s32[]{:T(128)}, f32[16,128]{1,0:T(8,128)S(1)}, ...), condition=%wide.region_12.0_spmd.clone, body=%wide.region_10.0_spmd.clone.sunk | while | flops 11439623 | bytes 186540 | solution.py:50
  213.4 1.1 convolution_add_fusion.5
  214.5 1.1 convolution_add_fusion.5
  215.7 1.1 convolution_add_fusion.5
  216.9 1.1 convolution_add_fusion.5
  218.0 1.1 convolution_add_fusion.5
  219.2 1.1 convolution_add_fusion.5
  220.4 1.1 convolution_add_fusion.5
  221.6 1.1 convolution_add_fusion.5
  222.9 36.9 %psum.38 = f32[16]{0:T(128)S(1)} all-reduce(f32[16]{0:T(128)S(1)} %multiply_reduce_fusion.7), channel_id=1, replica_groups=mesh['blk'=16,'grp'=2] {'blk','grp'}, use_global_device_ids=true, to_apply=%region_14.0 | all-reduce | flops 16 | bytes 128 | tf_op jit(solution)/shard_map/psum | solution.py:91
  259.7 0.7 fusion.68
  260.4 40.5 %all_gather.17 = bf16[16,4096]{1,0:T(8,128)(2,1)S(1)} all-gather(bf16[16,128]{1,0:T(8,128)(2,1)S(1)} %get-tuple-element.537), channel_id=1, replica_groups=mesh['blk'=16,'grp'=2] {'blk','grp'}, dimensions={1}, use_global_device_ids=true | all-gather | bytes 135168 | tf_op jit(solution)/shard_map/all_gather | solution.py:70
  301.6 11.2 %while.45 = (s32[]{:T(128)}, f32[32,128]{1,0:T(8,128)S(1)}, bf16[16,4096]{1,0:T(8,128)(2,1)S(1)}, f32[128]{0:T(128)S(1)}, bf16[64,4096]{1,0:T(8,128)(2,1)S(1)}, ...) while((s32[]{:T(128)}, f32[32,128]{1,0:T(8,128)S(1)}, ...), condition=%wide.region_17.0_spmd.clone, body=%wide.region_15.0_spmd.clone.sunk | while | flops 14003719 | bytes 1036997 | solution.py:50
  301.6 0.9 fusion.95
  302.6 0.2 fusion.97
  303.0 0.9 fusion.95
  304.0 0.2 fusion.97
  304.4 0.9 fusion.95
  305.4 0.2 fusion.97
  305.8 0.9 fusion.95
  306.8 0.2 fusion.97
  307.2 0.9 fusion.95
  308.2 0.2 fusion.97
  308.6 0.9 fusion.95
  309.6 0.2 fusion.97
  310.0 0.9 fusion.95
  311.0 0.2 fusion.97
  311.4 0.9 fusion.95
  312.4 0.2 fusion.97
  312.8 0.7 multiply_reduce_fusion.6
  313.5 1.9 pad_maximum_fusion
  315.4 36.8 %psum.39 = f32[3]{0:T(128)S(1)} all-reduce(f32[3]{0:T(128)S(1)} %pad_maximum_fusion), channel_id=1, replica_groups=mesh['blk'=16,'grp'=2] {'blk','grp'}, use_global_device_ids=true, to_apply=%region_21.22 | all-reduce | flops 3 | bytes 24 | tf_op jit(solution)/shard_map/psum | solution.py:114
  352.2 0.5 broadcast_multiply_fusion
  (60 shorter events, 3.1 us)
Async XLA Ops:
  0.6 44.9 %copy-start.1 = (bf16[64,128]{1,0:T(8,128)(2,1)S(1)}, bf16[64,128]{1,0:T(8,128)(2,1)}, u32[]{:S(2)}) copy-start(bf16[64,128]{1,0:T(8,128)(2,1)} %param.11) | copy-start | bytes 49156
  45.6 0.7 copy-start
  260.4 52.4 %copy-start.2 = (f32[16,128]{1,0:T(8,128)}, f32[16,128]{1,0:T(8,128)S(1)}, u32[]{:S(2)}) copy-start(f32[16,128]{1,0:T(8,128)S(1)} %get-tuple-element.538) | copy-start | bytes 24580
where the time goes:
time: 354 us; the launch traced here: 353 us
  blocking collectives  315 us (89%)
  matrix products  28.6 us (8%)
  other arithmetic  5.38 us (2%)
    all_gather x3, blocking collectives, kernel_product(): lax.all_gather(rounded, ('blk', 'grp'), axis=1, tiled=True)  117 us
    all_gather x1, blocking collectives, kernel_product(): lax.all_gather(points, ('blk', 'grp'), axis=1, tiled=True)  44.9 us
    psum x1, blocking collectives, local(): norm_next = lax.psum(jnp.sum(residual * residual, axis=1), ('blk', 'grp'))  42.4 us
    psum x1, blocking collectives, local(): norm_now = lax.psum(jnp.sum(residual * residual, axis=1), ('blk', 'grp'))  36.9 us
    psum x1, blocking collectives, local(): curvature = lax.psum(jnp.sum(direction * applied, axis=1), ('blk', 'grp'))  36.9 us
    psum x1, blocking collectives, local(): gradient = 0.5 * lax.psum(local_terms, ('blk', 'grp')) / total_points  36.8 us
    dot_general x32, matrix products, apply_columns(): lax.dot_general(tile_vectors, single, (((1,), (1,)), ((), ())), preferred...  21 us
    dot_general x8, matrix products, kernel_tiles(): lax.dot_general(own_points, tile_points, (((0,), (0,)), ((), ())), prefer...  7.56 us

commit v1 on v0

v1 whole, which is shorter than its diff:
```python
import functools
import math

import jax
import jax.numpy as jnp
from jax import lax
from jax.experimental import pallas as pl
from jax.experimental.pallas import tpu as pltpu
from jax.sharding import PartitionSpec as P

F32 = jnp.float32
BF16 = jnp.bfloat16
LOG2E = math.log2(math.e)
TINY = 1e-36
NT = (((1,), (1,)), ((), ()))


def _vmem(count):
    return [pl.BlockSpec(memory_space=pltpu.VMEM) for _ in range(count)]


def _smem():
    return pl.BlockSpec(memory_space=pltpu.SMEM)


def pack_kernel(points_ref, right_ref, out_ref):
    feats = points_ref.shape[0]
    cols = right_ref.shape[0]
    right = right_ref[...]
    high = right.astype(BF16)
    low = (right - high.astype(F32)).astype(BF16)
    points = points_ref[...]
    for peer in range(out_ref.shape[0]):
        out_ref[peer, 0:feats, :] = points
        out_ref[peer, feats : feats + cols, :] = high
        out_ref[peer, feats + cols : feats + 2 * cols, :] = low


def tile_kernel(part_count, pair, length_ref, points_ref, *refs):
    parts = refs[:part_count]
    tiles_ref, message_ref, first_ref = refs[part_count:]
    feats, own = points_ref.shape
    cols = first_ref.shape[0]
    scale = length_ref[0]
    per_dist = 5.0 / (scale * scale)
    slope = 1.0 / (3.0 * scale)
    own_points = points_ref[...].astype(F32).T
    own_squares = jnp.sum(own_points * own_points, axis=1, keepdims=True) * per_dist
    own_squares = jnp.broadcast_to(own_squares, (own, own))
    own_points = own_points.astype(BF16)

    total = jnp.zeros((cols, 2 * own), F32)
    base = 0
    for part in parts:
        steps = part.shape[0] // pair

        def one_pair(step, carried, part=part, base=base):
            vectors = []
            for side in range(pair):
                block = step * pair + side
                points = part[block, 0:feats, :]
                wide = points.astype(F32)
                squares = jnp.sum(wide * wide, axis=0, keepdims=True) * per_dist
                inner = jnp.dot(own_points, points, preferred_element_type=F32)
                reduced = jnp.maximum((own_squares + squares) - inner * (2.0 * per_dist), TINY)
                radius = reduced * lax.rsqrt(reduced)
                damping = jnp.exp2(radius * (-LOG2E))
                linear = 1.0 + radius
                kern = (linear + reduced * (1.0 / 3.0)) * damping
                dkern = (reduced * slope) * (linear * damping)
                lanes = pl.ds(side * own, own)
                tiles_ref[base + step, 0:own, lanes] = kern.astype(BF16)
                tiles_ref[base + step, own : 2 * own, lanes] = dkern.astype(BF16)
                vectors.append(part[block, feats : feats + cols, :])
            vectors = jnp.concatenate(vectors, axis=1) if pair > 1 else vectors[0]
            return carried + lax.dot_general(
                vectors, tiles_ref[base + step], NT, preferred_element_type=F32
            )

        total = lax.fori_loop(0, steps, one_pair, total, unroll=math.gcd(steps, 4))
        base += steps
    first_ref[...] = total
    product = total[:, 0:own]
    for peer in range(message_ref.shape[0]):
        message_ref[peer] = product


def to_lanes(column, slot):
    cols = column.shape[0]
    lanes = lax.broadcasted_iota(jnp.int32, (cols, 128), 1)
    rows = lax.broadcasted_iota(jnp.int32, (cols, 128), 0)
    return jnp.where(lanes == rows + slot * cols, jnp.broadcast_to(column, (cols, 128)), 0.0)


def from_lanes(row, slot, cols):
    lanes = lax.broadcasted_iota(jnp.int32, (cols, 128), 1)
    rows = lax.broadcasted_iota(jnp.int32, (cols, 128), 0)
    picked = jnp.where(lanes == rows + slot * cols, jnp.broadcast_to(row, (cols, 128)), 0.0)
    return jnp.sum(picked, axis=1, keepdims=True)


def lane_sum(values):
    return jnp.sum(values, axis=1, keepdims=True)


def second_kernel(part_count, pair, feats, scalars_ref, right_ref, first_ref, tiles_ref, *refs):
    vectors = refs[:part_count]
    products = refs[part_count : 2 * part_count]
    message_ref, direction_ref, residual_ref, applied_ref, columns_ref, wide_ref = refs[2 * part_count :]
    cols, own = right_ref.shape
    amplitude = scalars_ref[1]
    jitter = scalars_ref[2]
    zero = jnp.zeros((cols, own), F32)

    def right_block(part, block):
        high = vectors[part][block, feats : feats + cols, :].astype(F32)
        low = vectors[part][block, feats + cols : feats + 2 * cols, :].astype(F32)
        return high, low

    def added(sums):
        total = sums[0]
        for other in sums[1:]:
            total = [one + two for one, two in zip(total, other)]
        return [lane_sum(one) for one in total]

    sums = []
    for part in range(part_count):
        def first_pass(block, carried, part=part):
            high, low = right_block(part, block)
            right = high + low
            product = products[part][block]
            return [
                carried[0] + right * right,
                carried[1] + right * (amplitude * product + jitter * right),
                carried[2] + low * product,
            ]

        count = vectors[part].shape[0]
        sums.append(lax.fori_loop(0, count, first_pass, [zero] * 3, unroll=math.gcd(count, 4)))
    norm, curvature, low_first = added(sums)
    step = norm / curvature

    sums = []
    for part in range(part_count):
        def second_pass(block, carried, part=part):
            high, low = right_block(part, block)
            right = high + low
            product = products[part][block]
            residual = right - step * (amplitude * product + jitter * right)
            return [carried[0] + residual * residual]

        count = vectors[part].shape[0]
        sums.append(lax.fori_loop(0, count, second_pass, [zero], unroll=math.gcd(count, 4)))
    (norm_next,) = added(sums)
    turn = norm_next / norm

    sums = []
    total = jnp.zeros((cols, 2 * own), F32)
    base = 0
    for part in range(part_count):
        steps = vectors[part].shape[0] // pair

        def third_pass(index, carried, part=part, base=base):
            total, low_second, dots, squares = carried
            rounded = []
            for side in range(pair):
                block = index * pair + side
                high, low = right_block(part, block)
                right = high + low
                product = products[part][block]
                residual = right - step * (amplitude * product + jitter * right)
                direction = residual + turn * right
                narrow = direction.astype(BF16)
                rounded.append(narrow)
                wide_ref[base * pair + block] = direction
                low_second = low_second + (direction - narrow.astype(F32)) * product
                dots = dots + right * direction
                squares = squares + direction * direction
            rounded = jnp.concatenate(rounded, axis=1) if pair > 1 else rounded[0]
            total = total + lax.dot_general(
                rounded, tiles_ref[base + index], NT, preferred_element_type=F32
            )
            return total, low_second, dots, squares

        total, *rest = lax.fori_loop(
            0, steps, third_pass, (total, zero, zero, zero), unroll=math.gcd(steps, 4)
        )
        sums.append(rest)
        base += steps
    low_second, dots, squares = added(sums)

    right = right_ref[...]
    product = first_ref[:, 0:own]
    slope = first_ref[:, own : 2 * own]
    residual = right - step * (amplitude * product + jitter * right)
    direction = residual + turn * right
    product_next = total[:, 0:own]
    slope_next = total[:, own : 2 * own]
    applied = amplitude * product_next + jitter * direction
    direction_ref[...] = direction
    residual_ref[...] = residual
    applied_ref[...] = applied
    lanes = lax.broadcasted_iota(jnp.int32, (cols, 128), 1)
    kept = jnp.zeros((cols, 128), F32)
    for slot, column in enumerate([step, norm_next, norm, low_first, low_second, dots, squares]):
        kept = jnp.where(lanes == slot, jnp.broadcast_to(column, (cols, 128)), kept)
    columns_ref[...] = kept

    low = right - right.astype(BF16).astype(F32)
    low_direction = direction - direction.astype(BF16).astype(F32)
    partial = [
        direction * applied,
        low * product_next,
        right * slope,
        right * slope_next,
        direction * slope,
        direction * slope_next,
        low_direction * product_next,
    ]
    packed = jnp.zeros((cols, 128), F32)
    for slot, values in enumerate(partial):
        packed = packed + to_lanes(lane_sum(values), slot)
    packed = jnp.sum(packed, axis=0, keepdims=True)
    for peer in range(message_ref.shape[0]):
        message_ref[peer, 0:1, :] = packed
        message_ref[peer, 1:2, :] = product_next[0:1, :]


def last_kernel(
    part_count, feats, points_total, scalars_ref, place_ref, right_ref, direction_ref, residual_ref,
    applied_ref, columns_ref, wide_ref, received_ref, *refs
):
    vectors = refs[:part_count]
    products = refs[part_count : 2 * part_count]
    solution_ref, final_ref, gradient_ref = refs[2 * part_count :]
    cols, own = right_ref.shape
    amplitude = scalars_ref[1]
    device_count = received_ref.shape[0]

    def gather_sums(device, carried):
        return carried + received_ref[device, 0:1, :]

    sums = lax.fori_loop(
        0, device_count, gather_sums, jnp.zeros((1, 128), F32), unroll=math.gcd(device_count, 8)
    )
    curvature, low_next, right_slope, right_slope_next, slope_cross, slope_square, low_square = [
        from_lanes(sums, slot, cols) for slot in range(7)
    ]
    step, norm_next, norm, low_first, low_second, dots, squares = [
        columns_ref[:, slot : slot + 1] for slot in range(7)
    ]
    step_next = norm_next / curvature

    solution_ref[...] = step * right_ref[...] + step_next * direction_ref[...]
    final_ref[...] = residual_ref[...] - step_next * applied_ref[...]

    zero = jnp.zeros((cols, own), F32)
    row_zero = jnp.zeros((1, own), F32)
    sums = []
    base = 0
    for part in range(part_count):
        count = vectors[part].shape[0]

        def one_block(block, carried, part=part, base=base):
            whole, first_row = carried
            right = (
                vectors[part][block, feats : feats + cols, :].astype(F32)
                + vectors[part][block, feats + cols : feats + 2 * cols, :].astype(F32)
            )
            rounded = (step * right + step_next * wide_ref[base + block]).astype(BF16).astype(F32)
            source = block * part_count + (place_ref[0] + part) % part_count
            return (
                whole + products[part][block] * rounded,
                first_row + received_ref[source, 1:2, :] * rounded[0:1, :],
            )

        sums.append(lax.fori_loop(0, count, one_block, (zero, row_zero), unroll=math.gcd(count, 4)))
        base += count
    whole, first_row = sums[0]
    for other in sums[1:]:
        whole = whole + other[0]
        first_row = first_row + other[1]
    right_kernel = lane_sum(whole) + step * low_first + step_next * low_next
    direction_kernel = lane_sum(first_row) + (step * low_second + step_next * low_square)[0:1, :]
    right_slope_u = step * right_slope + step_next * right_slope_next
    direction_slope_u = step * slope_cross + step_next * slope_square
    right_u = step * norm + step_next * dots
    direction_u = step * dots + step_next * squares
    is_first = lax.broadcasted_iota(jnp.int32, (cols, 1), 0) == 0
    direction_kernel = jnp.broadcast_to(direction_kernel, (cols, 1))
    weight = jnp.where(is_first, 1.0, -1.0 / (cols - 1))
    forms = []
    for right_form, direction_form in (
        (amplitude * right_slope_u, amplitude * direction_slope_u),
        (right_kernel, direction_kernel),
        (right_u, direction_u),
    ):
        form = jnp.where(is_first, step * right_form + step_next * direction_form, right_form)
        forms.append(jnp.sum(weight * form, axis=0, keepdims=True) * (0.5 / points_total))
    lanes = lax.broadcasted_iota(jnp.int32, (1, 128), 1)
    gradient = jnp.zeros((1, 128), F32)
    for slot, form in enumerate(forms):
        gradient = jnp.where(lanes == slot, jnp.broadcast_to(form, (1, 128)), gradient)
    gradient_ref[...] = gradient


def spread(message, axes, mesh_shape):
    blocks = mesh_shape["blk"]
    pair = mesh_shape["grp"]
    if pair == 2:
        mine = lax.all_to_all(message, "blk", 0, 0, tiled=True)
        return [mine, lax.ppermute(mine, "grp", [(0, 1), (1, 0)])]
    return [lax.all_to_all(message, axes, 0, 0, tiled=True)]


def local(mesh_shape, points, right_side, lengthscale, outputscale, noise_level):
    axes = ("blk", "grp")
    feats, own = points.shape
    cols = right_side.shape[0]
    devices = mesh_shape["blk"] * mesh_shape["grp"]
    by_pairs = mesh_shape["grp"] == 2
    peers = mesh_shape["blk"] if by_pairs else devices
    part_count = 2 if by_pairs else 1
    pair = 2 if peers % 2 == 0 else 1
    scalars = jnp.concatenate([lengthscale, outputscale, noise_level])
    shape = jax.ShapeDtypeStruct

    message = pl.pallas_call(
        pack_kernel,
        out_shape=shape((peers, feats + 2 * cols, own), BF16),
        in_specs=_vmem(2),
        out_specs=_vmem(1)[0],
        name="pack",
    )(points, right_side)
    vectors = spread(message, axes, mesh_shape)

    tiles, message, first = pl.pallas_call(
        functools.partial(tile_kernel, part_count, pair),
        out_shape=(
            shape((devices // pair, 2 * own, pair * own), BF16),
            shape((peers, cols, own), F32),
            shape((cols, 2 * own), F32),
        ),
        in_specs=[_smem()] + _vmem(1 + part_count),
        out_specs=tuple(_vmem(3)),
        name="tiles",
    )(scalars, points, *vectors)
    products = spread(message, axes, mesh_shape)

    message, direction, residual, applied, columns, wide = pl.pallas_call(
        functools.partial(second_kernel, part_count, pair, feats),
        out_shape=(
            shape((devices, 2, own), F32),
            shape((cols, own), F32),
            shape((cols, own), F32),
            shape((cols, own), F32),
            shape((cols, 128), F32),
            shape((devices, cols, own), F32),
        ),
        in_specs=[_smem()] + _vmem(3 + 2 * part_count),
        out_specs=tuple(_vmem(6)),
        name="second",
    )(scalars, right_side, first, tiles, *vectors, *products)
    received = lax.all_to_all(message, axes, 0, 0, tiled=True)

    place = lax.axis_index("grp").astype(jnp.int32)[None]
    solution, final, gradient = pl.pallas_call(
        functools.partial(last_kernel, part_count, feats, float(own * devices)),
        out_shape=(
            shape((cols, own), F32),
            shape((cols, own), F32),
            shape((1, 128), F32),
        ),
        in_specs=[_smem(), _smem()] + _vmem(7 + 2 * part_count),
        out_specs=tuple(_vmem(3)),
        name="last",
    )(scalars, place, right_side, direction, residual, applied, columns, wide, received, *vectors, *products)
    return solution, final, gradient[0, 0:3]


def solution(mesh):
    whole = P(None, ("blk", "grp"))
    return jax.shard_map(
        functools.partial(local, dict(mesh.shape)),
        mesh=mesh,
        in_specs=(whole, whole, P(), P(), P()),
        out_specs=(whole, whole, P()),
        check_vma=False,
    )
```

time: 354 us -> 64.6 us (0.18)
  blocking collectives: 315 us -> 32.8 us
  matrix products: 28.6 us -> 0 us
  Pallas kernels: 0 us -> 13.8 us
  waiting for transfers between devices: 0 us -> 8.6 us
  other arithmetic: 5.38 us -> 0.59 us
    all_gather x4 -> x0, blocking collectives: 162 us -> none  [the longest x3 117 us: kernel_product(): lax.all_gather(rounded, ('blk', 'grp'), axis=1, tiled=True)]
    psum x4 -> x0, blocking collectives: 153 us -> none  [the longest x1 42.4 us: local(): norm_next = lax.psum(jnp.sum(residual * residual, axis=1), ('blk', 'grp'))]
    all_to_all x0 -> x2, blocking collectives: none -> 32.8 us  [spread(): mine = lax.all_to_all(message, 'blk', 0, 0, tiled=True)]
    dot_general x40 -> x0, matrix products: 28.6 us -> none  [the longest x32 21 us: apply_columns(): lax.dot_general(tile_vectors, single, (((1,), (1,)), ((), ())), preferred...]
    pallas_call x0 -> x4, Pallas kernels: none -> 13.8 us  [the longest x1 5.69 us: local(): pl.pallas_call(functools.partial(tile_kernel, part_count, pair), out_shap...]
    all_to_all x0 -> x1, waiting for transfers between devices: none -> 7.25 us  [local(): received = lax.all_to_all(message, axes, 0, 0, tiled=True)]
  transfers between devices with their start and end apart: 0 -> 3, of which waited for: 0 -> 2; matrix products, arithmetic and copies ran while one was open for 0% -> 1% of each run, Pallas kernels for 0% -> 0%
where the time goes in v1:
time: 64.6 us; the launch traced here: 64.1 us
  blocking collectives  32.8 us (51%)
  Pallas kernels  13.8 us (21%)
  waiting for transfers between devices  8.6 us (13%)
  local copies, waits for them, and re-layouts  3.14 us (5%)
  between operations  2.6 us (4%)
  starting transfers between devices  2.55 us (4%)
    all_to_all x2, blocking collectives, spread(): mine = lax.all_to_all(message, 'blk', 0, 0, tiled=True)  32.8 us
    all_to_all x1, waiting for transfers between devices, local(): received = lax.all_to_all(message, axes, 0, 0, tiled=True)  7.25 us
    pallas_call x1, Pallas kernels, local(): pl.pallas_call(functools.partial(tile_kernel, part_count, pair), out_shap...  5.69 us
    pallas_call x1, Pallas kernels, local(): pl.pallas_call(functools.partial(second_kernel, part_count, pair, feats),...  4.05 us
    pallas_call x1, Pallas kernels, local(): pl.pallas_call(functools.partial(last_kernel, part_count, feats, float(ow...  2.56 us
    all_to_all x1, starting transfers between devices, local(): received = lax.all_to_all(message, axes, 0, 0, tiled=True)  2.54 us
    unnamed x10, local copies, waits for them, and re-layouts  2.02 us
    pallas_call x1, Pallas kernels, local(): pl.pallas_call(pack_kernel, out_shape=shape((peers, feats + 2 * cols, own...  1.51 us
  transfers between devices with their start and end apart: 3, of which 2 were waited for; matrix products, arithmetic and copies ran while one was open for 1% of the time, Pallas kernels for 0%

profile of v1, /device:TPU:0, one launch (start us, length us, event | category | flops | bytes accessed | tf_op | source)
XLA Modules:
  0.0 64.1 jit_solution(9297353617895172134)
XLA Ops:
  0.6 1.5 %pack.1 = bf16[16,96,128]{2,1,0:T(8,128)(2,1)} custom-call(bf16[64,128]{1,0:T(8,128)(2,1)} %points_ref.3, f32[16,128]{1,0:T(8,128)} %right_ref.5), custom_call_target="tpu_custom_call" | custom-call | tf_op jit(solution)/shard_map/pack/pallas_call | solution.py:328
  2.1 21.0 %all_to_all.15.refs_0_ = bf16[16,96,128]{2,1,0:T(8,128)(2,1)S(1)} all-to-all(bf16[16,96,128]{2,1,0:T(8,128)(2,1)} %pack.1), channel_id=1, replica_groups=mesh['blk'=16,'grp'=2] {'blk'}, dimensions={0} | all-to-all | bytes 786432 | tf_op jit(solution)/shard_map/all_to_all | solution.py:311
  23.1 0.0 copy-start
  23.1 0.0 collective-permute-start
  25.0 0.6 pad_maximum_fusion.length_ref.scalars_ref
  25.6 0.0 collective-permute-done.refs_1_
  25.6 0.0 copy-done
  25.6 0.0 copy-start.1
  25.6 0.8 %copy-done.1 = bf16[16,96,128]{2,1,0:T(8,128)(2,1)} copy-done((bf16[16,96,128]{2,1,0:T(8,128)(2,1)}, bf16[16,96,128]{2,1,0:T(8,128)(2,1)S(1)}, u32[]{:S(2)}) %copy-start.1) | copy-done | bytes 393240
  26.4 5.7 %tiles.1 = (bf16[16,256,256]{2,1,0:T(8,128)(2,1)}, f32[16,16,128]{2,1,0:T(8,128)}, f32[16,256]{1,0:T(8,128)}) custom-call(f32[3]{0:T(128)} %pad_maximum_fusion.length_ref.scalars_ref, bf16[64,128]{1,0:T(8,128)(2,1)} %points_ref.3, bf16[16,96,128]{2,1,0:T(8,128)(2,1)} %copy-done, bf16[16,96,128]{2,1,0:T(8,128)(2,1)} %copy-done.1), custom_call_target="tpu_custom_call" | custom-call | tf_op jit(solution)/shard_map/tiles/pallas_call | solution.py:337
  32.1 11.9 %all_to_all.16.refs_2_ = f32[16,16,128]{2,1,0:T(8,128)S(1)} all-to-all(f32[16,16,128]{2,1,0:T(8,128)} %get-tuple-element.17), channel_id=1, replica_groups=mesh['blk'=16,'grp'=2] {'blk'}, dimensions={0} | all-to-all | bytes 262144 | tf_op jit(solution)/shard_map/all_to_all | solution.py:311
  44.0 0.0 copy-start.2
  44.0 0.0 collective-permute-start.1
  44.0 1.3 %collective-permute-done.1.refs_3_ = f32[16,16,128]{2,1,0:T(8,128)S(1)} collective-permute-done((f32[16,16,128]{2,1,0:T(8,128)S(1)}, f32[16,16,128]{2,1,0:T(8,128)S(1)}, u32[]{:S(2)}, u32[]{:S(2)}) %collective-permute-start.1) | collective-permute-done | bytes 131104 | tf_op jit(solution)/shard_map/ppermute | solution.py:312
  45.3 0.0 copy-start.3
  45.3 0.0 copy-done.2
  45.3 0.6 %copy-done.3 = f32[16,16,128]{2,1,0:T(8,128)} copy-done((f32[16,16,128]{2,1,0:T(8,128)}, f32[16,16,128]{2,1,0:T(8,128)S(1)}, u32[]{:S(2)}) %copy-start.3) | copy-done | bytes 131096
  46.0 4.0 %second.1 = (f32[32,2,128]{2,1,0:T(2,128)}, f32[16,128]{1,0:T(8,128)}, f32[16,128]{1,0:T(8,128)}, f32[16,128]{1,0:T(8,128)}, f32[16,128]{1,0:T(8,128)}, /*index=5*/f32[32,16,128]{2,1,0:T(8,128)}) custom-call(f32[3]{0:T(128)} %pad_maximum_fusion.length_ref.scalars_ref, f32[16,128]{1,0:T(8,128)} %right_ref.5, f32[16,256]{1,0:T(8,128)} %get-tuple-element.15.first_ref, ...), custom_call_target="tpu_custom_call" | custom-call | tf_op jit(solution)/shard_map/second/pallas_call | solution.py:350
  50.0 2.5 %all-to-all-start.2 = ((f32[32,2,128]{2,1,0:T(2,128)}), f32[32,2,128]{2,1,0:T(2,128)S(1)}, u32[]{:S(2)}, u32[]{:S(2)}) async-start(f32[32,2,128]{2,1,0:T(2,128)} %get-tuple-element.23), calls=%async_computation.2 | async-start | bytes 65536 | tf_op jit(solution)/shard_map/all_to_all | solution.py:364
  52.6 7.3 %all-to-all-done.2.received_ref = f32[32,2,128]{2,1,0:T(2,128)S(1)} async-done(((f32[32,2,128]{2,1,0:T(2,128)}), f32[32,2,128]{2,1,0:T(2,128)S(1)}, u32[]{:S(2)}, u32[]{:S(2)}) %all-to-all-start.2) | async-done | bytes 32800 | tf_op jit(solution)/shard_map/all_to_all | solution.py:364
  59.8 0.0 copy-start.4
  59.8 0.6 copy-done.4
  60.4 2.6 %last.1 = (f32[16,128]{1,0:T(8,128)}, f32[16,128]{1,0:T(8,128)}, f32[1,128]{1,0:T(1,128)}) custom-call(f32[3]{0:T(128)} %pad_maximum_fusion.length_ref.scalars_ref, s32[1]{0:T(128)} %bitcast.place_ref, f32[16,128]{1,0:T(8,128)} %right_ref.5, f32[16,128]{1,0:T(8,128)} %get-tuple-element.18.direction_ref, f32[16,128]{1,0:T(8,128)} %get-tuple-element.19.residual_ref, ...), custom_call_target="tpu_custom_call" | custom-call | tf_op jit(solution)/shard_map/last/pallas_call | solution.py:367
  63.0 1.1 %slice_bitcast_fusion = f32[3]{0:T(128)} fusion(f32[1,128]{1,0:T(1,128)} %get-tuple-element.26), kind=kLoop, calls=%fused_computation.1 | loop fusion | bytes 24 | tf_op jit(solution)/shard_map/squeeze | solution.py:378
Async XLA Ops:
  23.1 2.5 %copy-start = (bf16[16,96,128]{2,1,0:T(8,128)(2,1)}, bf16[16,96,128]{2,1,0:T(8,128)(2,1)S(1)}, u32[]{:S(2)}) copy-start(bf16[16,96,128]{2,1,0:T(8,128)(2,1)S(1)} %all_to_all.15.refs_0_) | copy-start | bytes 1179652
  23.1 2.5 %collective-permute-start = (bf16[16,96,128]{2,1,0:T(8,128)(2,1)S(1)}, bf16[16,96,128]{2,1,0:T(8,128)(2,1)S(1)}, u32[]{:S(2)}, u32[]{:S(2)}) collective-permute-start(bf16[16,96,128]{2,1,0:T(8,128)(2,1)S(1)} %all_to_all.15.refs_0_), channel_id=1, source_target_pairs={{0,1},{1,0},{2,3},{3,2},{4,5},{5,4},{6,7},{7,6},{8,9},{9,8},{10,11... | collective-permute-start | bytes 1179656 | tf_op jit(solution)/shard_map/ppermute | solution.py:312
  25.6 0.8 %copy-start.1 = (bf16[16,96,128]{2,1,0:T(8,128)(2,1)}, bf16[16,96,128]{2,1,0:T(8,128)(2,1)S(1)}, u32[]{:S(2)}) copy-start(bf16[16,96,128]{2,1,0:T(8,128)(2,1)S(1)} %collective-permute-done.refs_1_) | copy-start | bytes 1179652
  44.0 1.4 %copy-start.2 = (f32[16,16,128]{2,1,0:T(8,128)}, f32[16,16,128]{2,1,0:T(8,128)S(1)}, u32[]{:S(2)}) copy-start(f32[16,16,128]{2,1,0:T(8,128)S(1)} %all_to_all.16.refs_2_) | copy-start | bytes 393220
  44.0 1.3 %collective-permute-start.1 = (f32[16,16,128]{2,1,0:T(8,128)S(1)}, f32[16,16,128]{2,1,0:T(8,128)S(1)}, u32[]{:S(2)}, u32[]{:S(2)}) collective-permute-start(f32[16,16,128]{2,1,0:T(8,128)S(1)} %all_to_all.16.refs_2_), channel_id=1, source_target_pairs={{0,1},{1,0},{2,3},{3,2},{4,5},{5,4},{6,7},{7,6},{8,9},{9,8},{10,11... | collective-permute-start | bytes 393224 | tf_op jit(solution)/shard_map/ppermute | solution.py:312
  45.3 0.7 %copy-start.3 = (f32[16,16,128]{2,1,0:T(8,128)}, f32[16,16,128]{2,1,0:T(8,128)S(1)}, u32[]{:S(2)}) copy-start(f32[16,16,128]{2,1,0:T(8,128)S(1)} %collective-permute-done.1.refs_3_) | copy-start | bytes 393220
  50.0 9.8 %all-to-all-start.2 = ((f32[32,2,128]{2,1,0:T(2,128)}), f32[32,2,128]{2,1,0:T(2,128)S(1)}, u32[]{:S(2)}, u32[]{:S(2)}) async-start(f32[32,2,128]{2,1,0:T(2,128)} %get-tuple-element.23), calls=%async_computation.2 | async-start | bytes 65536 | tf_op jit(solution)/shard_map/all_to_all | solution.py:364
  59.8 0.6 copy-start.4

commit v2 on v1

--- a/solution.py
+++ b/solution.py
@@ -36,10 +36,11 @@
         out_ref[peer, feats + cols : feats + 2 * cols, :] = low
 
 
-def tile_kernel(part_count, pair, length_ref, points_ref, *refs):
+def tile_kernel(part_count, pair, with_message, length_ref, points_ref, *refs):
     parts = refs[:part_count]
-    tiles_ref, message_ref, first_ref = refs[part_count:]
+    tiles_ref, *outs = refs[part_count:]
     feats, own = points_ref.shape
+    first_ref = outs[-1]
     cols = first_ref.shape[0]
     scale = length_ref[0]
     per_dist = 5.0 / (scale * scale)
@@ -49,7 +50,7 @@
     own_squares = jnp.broadcast_to(own_squares, (own, own))
     own_points = own_points.astype(BF16)
 
-    total = jnp.zeros((cols, 2 * own), F32)
+    total = jnp.zeros((cols, own), F32)
     base = 0
     for part in parts:
         steps = part.shape[0] // pair
@@ -66,11 +67,11 @@
                 radius = reduced * lax.rsqrt(reduced)
                 damping = jnp.exp2(radius * (-LOG2E))
                 linear = 1.0 + radius
-                kern = (linear + reduced * (1.0 / 3.0)) * damping
-                dkern = (reduced * slope) * (linear * damping)
-                lanes = pl.ds(side * own, own)
-                tiles_ref[base + step, 0:own, lanes] = kern.astype(BF16)
-                tiles_ref[base + step, own : 2 * own, lanes] = dkern.astype(BF16)
+                if with_message:
+                    tile = (linear + reduced * (1.0 / 3.0)) * damping
+                else:
+                    tile = (reduced * slope) * (linear * damping)
+                tiles_ref[base + step, :, pl.ds(side * own, own)] = tile.astype(BF16)
                 vectors.append(part[block, feats : feats + cols, :])
             vectors = jnp.concatenate(vectors, axis=1) if pair > 1 else vectors[0]
             return carried + lax.dot_general(
@@ -80,9 +81,9 @@
         total = lax.fori_loop(0, steps, one_pair, total, unroll=math.gcd(steps, 4))
         base += steps
     first_ref[...] = total
-    product = total[:, 0:own]
-    for peer in range(message_ref.shape[0]):
-        message_ref[peer] = product
+    if with_message:
+        for peer in range(outs[0].shape[0]):
+            outs[0][peer] = total
 
 
 def to_lanes(column, slot):
@@ -103,13 +104,16 @@
     return jnp.sum(values, axis=1, keepdims=True)
 
 
-def second_kernel(part_count, pair, feats, scalars_ref, right_ref, first_ref, tiles_ref, *refs):
+def second_kernel(
+    part_count, pair, feats, amplitude_ref, jitter_ref, place_ref, right_ref, kernel_ref, slope_ref,
+    kern_ref, dkern_ref, products_ref, *refs
+):
     vectors = refs[:part_count]
-    products = refs[part_count : 2 * part_count]
-    message_ref, direction_ref, residual_ref, applied_ref, columns_ref, wide_ref = refs[2 * part_count :]
+    message_ref, direction_ref, residual_ref, applied_ref, columns_ref, wide_ref = refs[part_count:]
     cols, own = right_ref.shape
-    amplitude = scalars_ref[1]
-    jitter = scalars_ref[2]
+    amplitude = amplitude_ref[0]
+    jitter = jitter_ref[0]
+    place = place_ref[0]
     zero = jnp.zeros((cols, own), F32)
 
     def right_block(part, block):
@@ -128,7 +132,7 @@
         def first_pass(block, carried, part=part):
             high, low = right_block(part, block)
             right = high + low
-            product = products[part][block]
+            product = products_ref[block * part_count + (place + part) % part_count]
             return [
                 carried[0] + right * right,
                 carried[1] + right * (amplitude * product + jitter * right),
@@ -145,7 +149,7 @@
         def second_pass(block, carried, part=part):
             high, low = right_block(part, block)
             right = high + low
-            product = products[part][block]
+            product = products_ref[block * part_count + (place + part) % part_count]
             residual = right - step * (amplitude * product + jitter * right)
             return [carried[0] + residual * residual]
 
@@ -155,19 +159,20 @@
     turn = norm_next / norm
 
     sums = []
-    total = jnp.zeros((cols, 2 * own), F32)
     base = 0
+    total = zero
+    slopes = zero
     for part in range(part_count):
         steps = vectors[part].shape[0] // pair
 
         def third_pass(index, carried, part=part, base=base):
-            total, low_second, dots, squares = carried
+            total, slopes, low_second, dots, squares = carried
             rounded = []
             for side in range(pair):
                 block = index * pair + side
                 high, low = right_block(part, block)
                 right = high + low
-                product = products[part][block]
+                product = products_ref[block * part_count + (place + part) % part_count]
                 residual = right - step * (amplitude * product + jitter * right)
                 direction = residual + turn * right
                 narrow = direction.astype(BF16)
@@ -178,24 +183,27 @@
                 squares = squares + direction * direction
             rounded = jnp.concatenate(rounded, axis=1) if pair > 1 else rounded[0]
             total = total + lax.dot_general(
-                rounded, tiles_ref[base + index], NT, preferred_element_type=F32
+                rounded, kern_ref[base + index], NT, preferred_element_type=F32
             )
-            return total, low_second, dots, squares
-
-        total, *rest = lax.fori_loop(
-            0, steps, third_pass, (total, zero, zero, zero), unroll=math.gcd(steps, 4)
+            slopes = slopes + lax.dot_general(
+                rounded, dkern_ref[base + index], NT, preferred_element_type=F32
+            )
+            return total, slopes, low_second, dots, squares
+
+        total, slopes, *rest = lax.fori_loop(
+            0, steps, third_pass, (total, slopes, zero, zero, zero), unroll=math.gcd(steps, 4)
         )
         sums.append(rest)
         base += steps
     low_second, dots, squares = added(sums)
 
     right = right_ref[...]
-    product = first_ref[:, 0:own]
-    slope = first_ref[:, own : 2 * own]
+    product = kernel_ref[...]
+    slope = slope_ref[...]
     residual = right - step * (amplitude * product + jitter * right)
     direction = residual + turn * right
-    product_next = total[:, 0:own]
-    slope_next = total[:, own : 2 * own]
+    product_next = total
+    slope_next = slopes
     applied = amplitude * product_next + jitter * direction
     direction_ref[...] = direction
     residual_ref[...] = residual
@@ -227,14 +235,13 @@
 
 
 def last_kernel(
-    part_count, feats, points_total, scalars_ref, place_ref, right_ref, direction_ref, residual_ref,
-    applied_ref, columns_ref, wide_ref, received_ref, *refs
+    part_count, feats, points_total, amplitude_ref, place_ref, right_ref, direction_ref, residual_ref,
+    applied_ref, columns_ref, wide_ref, received_ref, products_ref, *refs
 ):
     vectors = refs[:part_count]
-    products = refs[part_count : 2 * part_count]
-    solution_ref, final_ref, gradient_ref = refs[2 * part_count :]
+    solution_ref, final_ref, gradient_ref = refs[part_count:]
     cols, own = right_ref.shape
-    amplitude = scalars_ref[1]
+    amplitude = amplitude_ref[0]
     device_count = received_ref.shape[0]
 
     def gather_sums(device, carried):
@@ -270,7 +277,7 @@
             rounded = (step * right + step_next * wide_ref[base + block]).astype(BF16).astype(F32)
             source = block * part_count + (place_ref[0] + part) % part_count
             return (
-                whole + products[part][block] * rounded,
+                whole + products_ref[source] * rounded,
                 first_row + received_ref[source, 1:2, :] * rounded[0:1, :],
             )
 
@@ -289,19 +296,13 @@
     is_first = lax.broadcasted_iota(jnp.int32, (cols, 1), 0) == 0
     direction_kernel = jnp.broadcast_to(direction_kernel, (cols, 1))
     weight = jnp.where(is_first, 1.0, -1.0 / (cols - 1))
-    forms = []
-    for right_form, direction_form in (
+    for slot, (right_form, direction_form) in enumerate((
         (amplitude * right_slope_u, amplitude * direction_slope_u),
         (right_kernel, direction_kernel),
         (right_u, direction_u),
-    ):
+    )):
         form = jnp.where(is_first, step * right_form + step_next * direction_form, right_form)
-        forms.append(jnp.sum(weight * form, axis=0, keepdims=True) * (0.5 / points_total))
-    lanes = lax.broadcasted_iota(jnp.int32, (1, 128), 1)
-    gradient = jnp.zeros((1, 128), F32)
-    for slot, form in enumerate(forms):
-        gradient = jnp.where(lanes == slot, jnp.broadcast_to(form, (1, 128)), gradient)
-    gradient_ref[...] = gradient
+        gradient_ref[slot] = jnp.sum(weight * form) * (0.5 / points_total)
 
 
 def spread(message, axes, mesh_shape):
@@ -322,8 +323,12 @@
     peers = mesh_shape["blk"] if by_pairs else devices
     part_count = 2 if by_pairs else 1
     pair = 2 if peers % 2 == 0 else 1
-    scalars = jnp.concatenate([lengthscale, outputscale, noise_level])
-    shape = jax.ShapeDtypeStruct
+    params = pltpu.CompilerParams(vmem_limit_bytes=(4 << 20) + devices * (40 << 10))
+    shape = pltpu.VMEM
+    result = jax.ShapeDtypeStruct
+
+    def near(*arrays):
+        return [pltpu.with_memory_space_constraint(array, pltpu.VMEM) for array in arrays]
 
     message = pl.pallas_call(
         pack_kernel,
@@ -331,22 +336,30 @@
         in_specs=_vmem(2),
         out_specs=_vmem(1)[0],
         name="pack",
+        compiler_params=params,
     )(points, right_side)
     vectors = spread(message, axes, mesh_shape)
 
-    tiles, message, first = pl.pallas_call(
-        functools.partial(tile_kernel, part_count, pair),
-        out_shape=(
-            shape((devices // pair, 2 * own, pair * own), BF16),
-            shape((peers, cols, own), F32),
-            shape((cols, 2 * own), F32),
-        ),
+    tile_shape = shape((devices // pair, own, pair * own), BF16)
+    kern, message, kernel_first = pl.pallas_call(
+        functools.partial(tile_kernel, part_count, pair, True),
+        out_shape=(tile_shape, shape((devices, cols, own), F32), shape((cols, own), F32)),
         in_specs=[_smem()] + _vmem(1 + part_count),
         out_specs=tuple(_vmem(3)),
-        name="tiles",
-    )(scalars, points, *vectors)
-    products = spread(message, axes, mesh_shape)
-
+        name="kern",
+        compiler_params=params,
+    )(lengthscale, points, *near(*vectors))
+    products = lax.all_to_all(message, axes, 0, 0, tiled=True)
+    dkern, slope_first = pl.pallas_call(
+        functools.partial(tile_kernel, part_count, pair, False),
+        out_shape=(tile_shape, shape((cols, own), F32)),
+        in_specs=[_smem()] + _vmem(1 + part_count),
+        out_specs=tuple(_vmem(2)),
+        name="dkern",
+        compiler_params=params,
+    )(lengthscale, points, *near(*vectors))
+
+    place = lax.axis_index("grp").astype(jnp.int32)[None]
     message, direction, residual, applied, columns, wide = pl.pallas_call(
         functools.partial(second_kernel, part_count, pair, feats),
         out_shape=(
@@ -357,25 +370,32 @@
             shape((cols, 128), F32),
             shape((devices, cols, own), F32),
         ),
-        in_specs=[_smem()] + _vmem(3 + 2 * part_count),
+        in_specs=[_smem()] * 3 + _vmem(6 + part_count),
         out_specs=tuple(_vmem(6)),
         name="second",
-    )(scalars, right_side, first, tiles, *vectors, *products)
+        compiler_params=params,
+    )(
+        outputscale, noise_level, place, right_side,
+        *near(kernel_first, slope_first, kern, dkern, products, *vectors),
+    )
     received = lax.all_to_all(message, axes, 0, 0, tiled=True)
 
-    place = lax.axis_index("grp").astype(jnp.int32)[None]
     solution, final, gradient = pl.pallas_call(
         functools.partial(last_kernel, part_count, feats, float(own * devices)),
         out_shape=(
-            shape((cols, own), F32),
-            shape((cols, own), F32),
-            shape((1, 128), F32),
+            result((cols, own), F32),
+            result((cols, own), F32),
+            result((3,), F32),
         ),
-        in_specs=[_smem(), _smem()] + _vmem(7 + 2 * part_count),
-        out_specs=tuple(_vmem(3)),
+        in_specs=[_smem(), _smem()] + _vmem(8 + part_count),
+        out_specs=tuple(_vmem(2) + [_smem()]),
         name="last",
-    )(scalars, place, right_side, direction, residual, applied, columns, wide, received, *vectors, *products)
-    return solution, final, gradient[0, 0:3]
+        compiler_params=params,
+    )(
+        outputscale, place, right_side,
+        *near(direction, residual, applied, columns, wide, received, products, *vectors),
+    )
+    return solution, final, gradient
 
 
 def solution(mesh):

time: 64.6 us -> 53.4 us (0.83)
  Pallas kernels: 13.8 us -> 7.98 us
  blocking collectives: 32.8 us -> 30.2 us
  local copies, waits for them, and re-layouts: 3.14 us -> 1.42 us
    all_to_all x2 -> x1, blocking collectives: 32.8 us -> 20.8 us  [spread(): mine = lax.all_to_all(message, 'blk', 0, 0, tiled=True)]
    all_to_all x0 -> x1, blocking collectives: none -> 9.45 us  [local(): received = lax.all_to_all(message, axes, 0, 0, tiled=True)]
    pallas_call x1, Pallas kernels: 4.05 us -> 1.55 us  [local(): pl.pallas_call(functools.partial(second_kernel, part_count, pair, feats),...]
    pallas_call x1, Pallas kernels: 1.51 us -> 0.04 us  [local(): pl.pallas_call(pack_kernel, out_shape=shape((peers, feats + 2 * cols, own...]
    pallas_call x1, Pallas kernels: 2.56 us -> 1.25 us  [local(): pl.pallas_call(functools.partial(last_kernel, part_count, feats, float(ow...]
    squeeze x1 -> x0, local copies, waits for them, and re-layouts: 1.12 us -> none  [local(): return (solution, final, gradient[0, 0:3])]
    unnamed x10 -> x8, local copies, waits for them, and re-layouts: 2.02 us -> 1.42 us
    pallas_call x1 -> x2, Pallas kernels: 5.69 us -> 5.14 us  [the longest x1 2.93 us: local(): pl.pallas_call(functools.partial(tile_kernel, part_count, pair, True), ou...]
  transfers between devices with their start and end apart: 3 -> 2, of which waited for: 2 -> 2; matrix products, arithmetic and copies ran while one was open for 1% -> 0% of each run, Pallas kernels for 0% -> 4%
where the time goes in v2:
time: 53.4 us; the launch traced here: 53 us
  blocking collectives  30.2 us (57%)
  waiting for transfers between devices  8.13 us (15%)
  Pallas kernels  7.98 us (15%)
  between operations  2.62 us (5%)
  starting transfers between devices  2.59 us (5%)
  local copies, waits for them, and re-layouts  1.42 us (3%)
    all_to_all x1, blocking collectives, spread(): mine = lax.all_to_all(message, 'blk', 0, 0, tiled=True)  20.8 us
    all_to_all x1, blocking collectives, local(): received = lax.all_to_all(message, axes, 0, 0, tiled=True)  9.45 us
    all_to_all x1, waiting for transfers between devices, local(): products = lax.all_to_all(message, axes, 0, 0, tiled=True)  7.06 us
    pallas_call x1, Pallas kernels, local(): pl.pallas_call(functools.partial(tile_kernel, part_count, pair, True), ou...  2.93 us
    all_to_all x1, starting transfers between devices, local(): products = lax.all_to_all(message, axes, 0, 0, tiled=True)  2.59 us
    pallas_call x1, Pallas kernels, local(): pl.pallas_call(functools.partial(tile_kernel, part_count, pair, False), o...  2.21 us
    pallas_call x1, Pallas kernels, local(): pl.pallas_call(functools.partial(second_kernel, part_count, pair, feats),...  1.55 us
    unnamed x8, local copies, waits for them, and re-layouts  1.42 us
  transfers between devices with their start and end apart: 2, of which 2 were waited for; matrix products, arithmetic and copies ran while one was open for 0% of the time, Pallas kernels for 4%

profile of v2, /device:TPU:0, one launch (start us, length us, event | category | flops | bytes accessed | tf_op | source)
XLA Modules:
  0.0 53.0 jit_solution(10321343196013335875)
XLA Ops:
  0.6 0.0 copy-start
  0.6 0.7 %copy-done = bf16[64,128]{1,0:T(8,128)(2,1)S(1)} copy-done((bf16[64,128]{1,0:T(8,128)(2,1)S(1)}, bf16[64,128]{1,0:T(8,128)(2,1)}, u32[]{:S(2)}) %copy-start) | copy-done | bytes 16408
  1.4 0.0 copy-start.2
  1.4 0.7 %copy-done.2 = f32[16,128]{1,0:T(8,128)S(1)} copy-done((f32[16,128]{1,0:T(8,128)S(1)}, f32[16,128]{1,0:T(8,128)}, u32[]{:S(2)}) %copy-start.2) | copy-done | bytes 8216
  2.1 0.0 copy-start.1
  2.1 20.8 %all_to_all.15.refs_0_ = bf16[16,96,128]{2,1,0:T(8,128)(2,1)S(1)} all-to-all(bf16[16,96,128]{2,1,0:T(8,128)(2,1)S(1)} %pack.1), channel_id=1, replica_groups=mesh['blk'=16,'grp'=2] {'blk'}, dimensions={0} | all-to-all | bytes 786432 | tf_op jit(solution)/shard_map/all_to_all | solution.py:312
  22.9 0.0 collective-permute-start
  23.5 1.1 %collective-permute-done.refs_1_ = bf16[16,96,128]{2,1,0:T(8,128)(2,1)S(1)} collective-permute-done((bf16[16,96,128]{2,1,0:T(8,128)(2,1)S(1)}, bf16[16,96,128]{2,1,0:T(8,128)(2,1)S(1)}, u32[]{:S(2)}, u32[]{:S(2)}) %collective-permute-start) | collective-permute-done | bytes 393248 | tf_op jit(solution)/shard_map/ppermute | solution.py:313
  24.6 0.0 copy-done.1
  24.6 2.9 %kern.1 = (bf16[16,128,256]{2,1,0:T(8,128)(2,1)S(1)}, f32[32,16,128]{2,1,0:T(8,128)}, f32[16,128]{1,0:T(8,128)S(1)}) custom-call(f32[1]{0:T(128)S(6)} %copy.8.length_ref, bf16[64,128]{1,0:T(8,128)(2,1)S(1)} %copy-done.1, bf16[16,96,128]{2,1,0:T(8,128)(2,1)S(1)} %all_to_all.15.refs_0_, bf16[16,96,128]{2,1,0:T(8,128)(2,1)S(1)} %collective-permute-done.refs_1_), custom_call_target="tpu_custom_call" | custom-call | tf_op jit(solution)/shard_map/kern/pallas_call | solution.py:344
  27.5 2.6 %all-to-all-start.1 = ((f32[32,16,128]{2,1,0:T(8,128)}), f32[32,16,128]{2,1,0:T(8,128)S(1)}, u32[]{:S(2)}, u32[]{:S(2)}) async-start(f32[32,16,128]{2,1,0:T(8,128)} %get-tuple-element.18), calls=%async_computation.1 | async-start | bytes 524288 | tf_op jit(solution)/shard_map/all_to_all | solution.py:352
  31.4 2.2 %dkern.1 = (bf16[16,128,256]{2,1,0:T(8,128)(2,1)S(1)}, f32[16,128]{1,0:T(8,128)S(1)}) custom-call(f32[1]{0:T(128)S(6)} %copy.8.length_ref, bf16[64,128]{1,0:T(8,128)(2,1)S(1)} %copy-done.1, bf16[16,96,128]{2,1,0:T(8,128)(2,1)S(1)} %all_to_all.15.refs_0_, bf16[16,96,128]{2,1,0:T(8,128)(2,1)S(1)} %collective-permute-done.refs_1_), custom_call_target="tpu_custom_call" | custom-call | tf_op jit(solution)/shard_map/dkern/pallas_call | solution.py:353
  33.6 0.0 copy-start.3
  33.6 7.1 %all-to-all-done.1.products_ref = f32[32,16,128]{2,1,0:T(8,128)S(1)} async-done(((f32[32,16,128]{2,1,0:T(8,128)}), f32[32,16,128]{2,1,0:T(8,128)S(1)}, u32[]{:S(2)}, u32[]{:S(2)}) %all-to-all-start.1) | async-done | bytes 262176 | tf_op jit(solution)/shard_map/all_to_all | solution.py:352
  40.7 0.0 copy-done.3
  40.7 1.6 %second.1 = (f32[32,2,128]{2,1,0:T(2,128)S(1)}, f32[16,128]{1,0:T(8,128)S(1)}, f32[16,128]{1,0:T(8,128)S(1)}, f32[16,128]{1,0:T(8,128)S(1)}, f32[16,128]{1,0:T(8,128)S(1)}, /*index=5*/f32[32,16,128]{2,1,0:T(8,128)S(1)}) custom-call(f32[1]{0:T(128)S(6)} %copy.9.amplitude_ref, f32[1]{0:T(128)S(6)} %copy.10.jitter_ref, s32[1]{0:T(128)} %bitcast.place_ref, ...), custom_call_target="tpu_custom_call" | custom-call | tf_op jit(solution)/shard_map/second/pallas_call | solution.py:363
  42.3 9.5 %all_to_all.16.received_ref = f32[32,2,128]{2,1,0:T(2,128)S(1)} all-to-all(f32[32,2,128]{2,1,0:T(2,128)S(1)} %get-tuple-element.24), channel_id=1, replica_groups=mesh['blk'=16,'grp'=2] {'blk','grp'}, dimensions={0} | all-to-all | bytes 65536 | tf_op jit(solution)/shard_map/all_to_all | solution.py:381
  51.7 1.2 %last.1 = (f32[16,128]{1,0:T(8,128)}, f32[16,128]{1,0:T(8,128)}, f32[3]{0:T(128)}) custom-call(f32[1]{0:T(128)S(6)} %copy.9.amplitude_ref, s32[1]{0:T(128)} %bitcast.place_ref, f32[16,128]{1,0:T(8,128)S(1)} %copy-done.3, f32[16,128]{1,0:T(8,128)S(1)} %get-tuple-element.19.direction_ref, f32[16,128]{1,0:T(8,128)S(1)} %get-tuple-element.20.residual_ref, ...), custom_call_target="tpu_custom_call" | custom-call | tf_op jit(solution)/shard_map/last/pallas_call | solution.py:383
  (1 shorter events, 0.0 us)
Async XLA Ops:
  0.6 0.7 %copy-start = (bf16[64,128]{1,0:T(8,128)(2,1)S(1)}, bf16[64,128]{1,0:T(8,128)(2,1)}, u32[]{:S(2)}) copy-start(bf16[64,128]{1,0:T(8,128)(2,1)} %points_ref.5) | copy-start | bytes 49156
  1.4 0.7 %copy-start.2 = (f32[16,128]{1,0:T(8,128)S(1)}, f32[16,128]{1,0:T(8,128)}, u32[]{:S(2)}) copy-start(f32[16,128]{1,0:T(8,128)} %right_ref.5) | copy-start | bytes 24580
  2.1 22.5 %copy-start.1 = (bf16[64,128]{1,0:T(8,128)(2,1)S(1)}, bf16[64,128]{1,0:T(8,128)(2,1)}, u32[]{:S(2)}) copy-start(bf16[64,128]{1,0:T(8,128)(2,1)} %points_ref.5) | copy-start | bytes 49156
  22.9 1.7 %collective-permute-start = (bf16[16,96,128]{2,1,0:T(8,128)(2,1)S(1)}, bf16[16,96,128]{2,1,0:T(8,128)(2,1)S(1)}, u32[]{:S(2)}, u32[]{:S(2)}) collective-permute-start(bf16[16,96,128]{2,1,0:T(8,128)(2,1)S(1)} %all_to_all.15.refs_0_), channel_id=1, source_target_pairs={{0,1},{1,0},{2,3},{3,2},{4,5},{5,4},{6,7},{7,6},{8,9},{9,8},{10,11... | collective-permute-start | bytes 1179656 | tf_op jit(solution)/shard_map/ppermute | solution.py:313
  27.5 13.2 %all-to-all-start.1 = ((f32[32,16,128]{2,1,0:T(8,128)}), f32[32,16,128]{2,1,0:T(8,128)S(1)}, u32[]{:S(2)}, u32[]{:S(2)}) async-start(f32[32,16,128]{2,1,0:T(8,128)} %get-tuple-element.18), calls=%async_computation.1 | async-start | bytes 524288 | tf_op jit(solution)/shard_map/all_to_all | solution.py:352
  33.6 7.1 %copy-start.3 = (f32[16,128]{1,0:T(8,128)S(1)}, f32[16,128]{1,0:T(8,128)}, u32[]{:S(2)}) copy-start(f32[16,128]{1,0:T(8,128)} %right_ref.5) | copy-start | bytes 24580

commit v3 on v2

v3 whole, which is shorter than its diff:
```python
import functools
import math

import jax
import jax.numpy as jnp
from jax import lax
from jax.experimental import pallas as pl
from jax.experimental.pallas import tpu as pltpu
from jax.sharding import PartitionSpec as P

F32 = jnp.float32
BF16 = jnp.bfloat16
LOG2E = math.log2(math.e)
TINY = 1e-36
NT = (((1,), (1,)), ((), ()))


def _vmem(count):
    return [pl.BlockSpec(memory_space=pltpu.VMEM) for _ in range(count)]


def _smem():
    return pl.BlockSpec(memory_space=pltpu.SMEM)


def _hbm(count):
    return [pl.BlockSpec(memory_space=pltpu.HBM) for _ in range(count)]


def lane_sum(values):
    return jnp.sum(values, axis=1, keepdims=True)


def unrolled(count, most):
    return max(divisor for divisor in range(1, most + 1) if count % divisor == 0)


def pack_kernel(points_hbm, right_hbm, out_ref, points_ref, right_ref, sems):
    feats = points_ref.shape[0]
    cols = right_ref.shape[0]
    copies = [
        pltpu.make_async_copy(right_hbm, right_ref, sems.at[0]),
        pltpu.make_async_copy(points_hbm, points_ref, sems.at[1]),
    ]
    for copy in copies:
        copy.start()
    copies[0].wait()
    right = right_ref[...]
    high = right.astype(BF16)
    low = (right - high.astype(F32)).astype(BF16)
    for peer in range(out_ref.shape[0]):
        out_ref[peer, feats : feats + cols, :] = high
        out_ref[peer, feats + cols : feats + 2 * cols, :] = low
    copies[1].wait()
    points = points_ref[...]
    for peer in range(out_ref.shape[0]):
        out_ref[peer, 0:feats, :] = points


class Distances:
    def __init__(self, length_ref, points_ref):
        scale = length_ref[0]
        self.scale = scale
        self.factor = (5.0 * LOG2E * LOG2E) / (scale * scale)
        own = points_ref.shape[1]
        points = points_ref[...].astype(F32).T
        squares = jnp.sum(points * points, axis=1, keepdims=True) * self.factor
        self.squares = jnp.broadcast_to(squares, (own, own))
        self.points = (-2.0 * points).astype(BF16)

    def __call__(self, points):
        wide = points.astype(F32)
        squares = jnp.sum(wide * wide, axis=0, keepdims=True) * self.factor
        inner = jnp.dot(self.points, points, preferred_element_type=F32)
        reduced = jnp.maximum((self.squares + squares) + inner * self.factor, TINY)
        return reduced, reduced * lax.rsqrt(reduced)


def kern_tile(reduced, root):
    shifted = root + 1.5 * LOG2E
    return (shifted * shifted + 0.75 * LOG2E * LOG2E) * jnp.exp2(-math.log2(3.0 * LOG2E * LOG2E) - root)


def kern_kernel(pair, has_before, length_ref, points_ref, part_ref, *refs):
    before = refs[0][...] if has_before else None
    tiles_ref, *outs = refs[1 if has_before else 0 :]
    feats, own = points_ref.shape
    total_ref = outs[0]
    cols = total_ref.shape[0]
    distances = Distances(length_ref, points_ref)
    steps = part_ref.shape[0] // pair
    total = before if has_before else jnp.zeros((cols, own), F32)

    def one_pair(step, total):
        vectors = []
        for side in range(pair):
            block = step * pair + side
            tile = kern_tile(*distances(part_ref[block, 0:feats, :]))
            tiles_ref[step, :, pl.ds(side * own, own)] = tile.astype(BF16)
            vectors.append(part_ref[block, feats : feats + cols, :])
        vectors = jnp.concatenate(vectors, axis=1) if pair > 1 else vectors[0]
        return total + lax.dot_general(vectors, tiles_ref[step], NT, preferred_element_type=F32)

    total = lax.fori_loop(0, steps, one_pair, total, unroll=unrolled(steps, 8))
    total_ref[...] = total
    if len(outs) > 1:
        message_ref = outs[1]
        rows = message_ref.shape[1]
        for peer in range(message_ref.shape[0]):
            first = (peer * rows) % cols
            message_ref[peer] = total[first : first + rows]


def dkern_kernel(
    part_count, pair, length_ref, amplitude_ref, jitter_ref, points_ref, *refs
):
    parts = refs[:part_count]
    tiles_ref, total_ref, wide_ref, norm_ref, scalars_ref = refs[part_count:]
    for slot, scalar in enumerate((amplitude_ref, jitter_ref)):
        scalars_ref[slot : slot + 1, :] = jnp.full((1, 128), scalar[0], F32)
    feats, own = points_ref.shape
    cols = total_ref.shape[0]
    distances = Distances(length_ref, points_ref)
    slope = 1.0 / (3.0 * LOG2E * LOG2E * LOG2E * distances.scale)
    total = jnp.zeros((cols, own), F32)
    norms = []
    base = 0
    for part in parts:
        steps = part.shape[0] // pair

        def one_pair(step, carried, part=part, base=base):
            total, norm = carried
            vectors = []
            for side in range(pair):
                block = step * pair + side
                reduced, root = distances(part[block, 0:feats, :])
                tile = (reduced * slope) * ((root + LOG2E) * jnp.exp2(-root))
                tiles_ref[base + step, :, pl.ds(side * own, own)] = tile.astype(BF16)
                high = part[block, feats : feats + cols, :]
                right = high.astype(F32) + part[block, feats + cols : feats + 2 * cols, :].astype(F32)
                wide_ref[base * pair + block] = right
                norm = norm + right * right
                vectors.append(high)
            vectors = jnp.concatenate(vectors, axis=1) if pair > 1 else vectors[0]
            total = total + lax.dot_general(
                vectors, tiles_ref[base + step], NT, preferred_element_type=F32
            )
            return total, norm

        total, norm = lax.fori_loop(
            0, steps, one_pair, (total, jnp.zeros((cols, own), F32)), unroll=unrolled(steps, 4)
        )
        norms.append(norm)
        base += steps
    total_ref[...] = total
    norm_ref[...] = jnp.broadcast_to(lane_sum(functools.reduce(jnp.add, norms)), norm_ref.shape)


def to_lanes(column, slot):
    cols = column.shape[0]
    lanes = lax.broadcasted_iota(jnp.int32, (cols, 128), 1)
    rows = lax.broadcasted_iota(jnp.int32, (cols, 128), 0)
    return jnp.where(lanes == rows + slot * cols, jnp.broadcast_to(column, (cols, 128)), 0.0)


def from_lanes(row, slot, cols):
    lanes = lax.broadcasted_iota(jnp.int32, (cols, 128), 1)
    rows = lax.broadcasted_iota(jnp.int32, (cols, 128), 0)
    picked = jnp.where(lanes == rows + slot * cols, jnp.broadcast_to(row, (cols, 128)), 0.0)
    return lane_sum(picked)


def into_columns(columns, cols):
    lanes = lax.broadcasted_iota(jnp.int32, (cols, 128), 1)
    kept = jnp.zeros((cols, 128), F32)
    for slot, column in enumerate(columns):
        kept = jnp.where(lanes == slot, jnp.broadcast_to(column, (cols, 128)), kept)
    return kept


def second_kernel(
    part_count, pair, halves, place_ref, scalars_ref, right_ref, kernel_ref, slope_ref,
    dkern_ref, wide_ref, norm_ref, *refs
):
    kerns = refs[:part_count]
    received = refs[part_count : part_count + halves]
    (
        message_ref, direction_ref, residual_ref, applied_ref, columns_ref, products_ref, turned_ref,
    ) = refs[part_count + halves :]
    cols, own = right_ref.shape
    amplitude = scalars_ref[0:1, :]
    jitter = scalars_ref[1:2, :]
    place = place_ref[0]
    zero = jnp.zeros((cols, own), F32)
    norm = norm_ref[:, 0:1]
    count = kerns[0].shape[0] * pair

    sums = []
    for part in range(part_count):
        def first_pass(block, carried, part=part):
            source = block * part_count + (place + part) % part_count
            if halves == 2:
                mine = received[0][source]
                other = received[1][source]
                product = jnp.concatenate(
                    [jnp.where(place == 0, mine, other), jnp.where(place == 0, other, mine)], axis=0
                )
            else:
                product = received[0][source]
            products_ref[part * count + block] = product
            right = wide_ref[part * count + block]
            applied = amplitude * product + jitter * right
            return carried[0] + right * applied, carried[1] + applied * applied

        sums.append(lax.fori_loop(0, count, first_pass, (zero, zero), unroll=unrolled(count, 8)))
    curvature, length = [lane_sum(functools.reduce(jnp.add, parts)) for parts in zip(*sums)]
    step = norm / curvature
    turn = (step * step * length - norm) / norm

    sums = []
    total = zero
    slopes = zero
    for part in range(part_count):
        base = part * (count // pair)

        def second_pass(index, carried, part=part, base=base):
            total, slopes, norms = carried
            rounded = []
            for side in range(pair):
                block = part * count + index * pair + side
                right = wide_ref[block]
                residual = right - step * (amplitude * products_ref[block] + jitter * right)
                direction = residual + turn * right
                turned_ref[block] = direction
                norms = norms + residual * residual
                rounded.append(direction)
            rounded = jnp.concatenate(rounded, axis=1) if pair > 1 else rounded[0]
            rounded = rounded.astype(BF16)
            total = total + lax.dot_general(
                rounded, kerns[part][index], NT, preferred_element_type=F32
            )
            slopes = slopes + lax.dot_general(
                rounded, dkern_ref[base + index], NT, preferred_element_type=F32
            )
            return total, slopes, norms

        total, slopes, norms = lax.fori_loop(
            0, count // pair, second_pass, (total, slopes, zero), unroll=unrolled(count // pair, 8)
        )
        sums.append(norms)
    norm_next = lane_sum(functools.reduce(jnp.add, sums))

    right = right_ref[...]
    residual = right - step * (amplitude * kernel_ref[...] + jitter * right)
    direction = residual + turn * right
    applied = amplitude * total + jitter * direction
    direction_ref[...] = direction
    residual_ref[...] = residual
    applied_ref[...] = applied
    columns_ref[...] = into_columns([step, norm_next, norm], cols)

    low = right - right.astype(BF16).astype(F32)
    low_direction = direction - direction.astype(BF16).astype(F32)
    slope = slope_ref[...]
    packed = jnp.zeros((cols, 128), F32)
    for slot, values in enumerate([
        direction * applied,
        low * total,
        right * slope,
        right * slopes,
        direction * slope,
        direction * slopes,
        low_direction * total,
    ]):
        packed = packed + to_lanes(lane_sum(values), slot)
    packed = jnp.sum(packed, axis=0, keepdims=True)
    for peer in range(message_ref.shape[0]):
        message_ref[peer, 0:1, :] = packed
        message_ref[peer, 1:2, :] = total[0:1, :]


def middle_kernel(part_count, wide_ref, products_ref, turned_ref, out_ref):
    blocks, cols, own = wide_ref.shape
    count = blocks // part_count
    zero = jnp.zeros((cols, own), F32)
    sums = []
    for part in range(part_count):
        def one_block(block, carried, part=part):
            block = part * count + block
            right = wide_ref[block]
            direction = turned_ref[block]
            product = products_ref[block]
            low = right - right.astype(BF16).astype(F32)
            low_direction = direction - direction.astype(BF16).astype(F32)
            return (
                carried[0] + low * product,
                carried[1] + low_direction * product,
                carried[2] + right * direction,
                carried[3] + direction * direction,
            )

        sums.append(lax.fori_loop(0, count, one_block, (zero,) * 4, unroll=unrolled(count, 4)))
    sums = [lane_sum(functools.reduce(jnp.add, parts)) for parts in zip(*sums)]
    out_ref[...] = into_columns(sums, cols)


def last_kernel(
    part_count, points_total, place_ref, scalars_ref, right_ref, direction_ref, residual_ref,
    applied_ref, columns_ref, middle_ref, wide_ref, products_ref, turned_ref, received_ref,
    solution_hbm, final_hbm, gradient_ref, solution_ref, final_ref, sems
):
    cols, own = right_ref.shape
    amplitude = scalars_ref[0:1, :]
    place = place_ref[0]
    devices = received_ref.shape[0]

    def gather_sums(device, carried):
        return carried + received_ref[device, 0:1, :]

    sums = lax.fori_loop(
        0, devices, gather_sums, jnp.zeros((1, 128), F32), unroll=unrolled(devices, 32)
    )
    step, norm_next, norm = [columns_ref[:, slot : slot + 1] for slot in range(3)]
    step_next = norm_next / from_lanes(sums, 0, cols)

    solution_ref[...] = step * right_ref[...] + step_next * direction_ref[...]
    final_ref[...] = residual_ref[...] - step_next * applied_ref[...]
    copies = [
        pltpu.make_async_copy(solution_ref, solution_hbm, sems.at[0]),
        pltpu.make_async_copy(final_ref, final_hbm, sems.at[1]),
    ]
    for copy in copies:
        copy.start()

    low_next, right_slope, right_slope_next, slope_cross, slope_square, low_square = [
        from_lanes(sums, slot, cols) for slot in range(1, 7)
    ]
    low_first, low_second, dots, squares = [middle_ref[:, slot : slot + 1] for slot in range(4)]
    count = wide_ref.shape[0] // part_count
    zero = jnp.zeros((cols, own), F32)
    row_zero = jnp.zeros((1, own), F32)
    sums = []
    for part in range(part_count):
        def one_block(index, carried, part=part):
            whole, first_row = carried
            block = part * count + index
            rounded = (step * wide_ref[block] + step_next * turned_ref[block]).astype(BF16).astype(F32)
            source = index * part_count + (place + part) % part_count
            return (
                whole + products_ref[block] * rounded,
                first_row + received_ref[source, 1:2, :] * rounded[0:1, :],
            )

        sums.append(lax.fori_loop(0, count, one_block, (zero, row_zero), unroll=unrolled(count, 8)))
    whole, first_row = [functools.reduce(jnp.add, parts) for parts in zip(*sums)]
    right_kernel = lane_sum(whole) + step * low_first + step_next * low_next
    direction_kernel = lane_sum(first_row) + (step * low_second + step_next * low_square)[0:1, :]
    is_first = lax.broadcasted_iota(jnp.int32, (cols, 1), 0) == 0
    weight = jnp.where(is_first, 1.0, -1.0 / (cols - 1))
    for slot, (right_form, direction_form) in enumerate((
        (
            amplitude[:, 0:1] * (step * right_slope + step_next * right_slope_next),
            amplitude[:, 0:1] * (step * slope_cross + step_next * slope_square),
        ),
        (right_kernel, jnp.broadcast_to(direction_kernel, (cols, 1))),
        (step * norm + step_next * dots, step * dots + step_next * squares),
    )):
        form = jnp.where(is_first, step * right_form + step_next * direction_form, right_form)
        gradient_ref[slot] = jnp.sum(weight * form) * (0.5 / points_total)
    for copy in copies:
        copy.wait()


SWAP = [(0, 1), (1, 0)]


def local(mesh_shape, points, right_side, lengthscale, outputscale, noise_level):
    axes = ("blk", "grp")
    feats, own = points.shape
    cols = right_side.shape[0]
    devices = mesh_shape["blk"] * mesh_shape["grp"]
    paired = mesh_shape["grp"] == 2
    peers = mesh_shape["blk"] if paired else devices
    part_count = 2 if paired else 1
    pair = 2 if peers % 2 == 0 else 1
    params = pltpu.CompilerParams(vmem_limit_bytes=(4 << 20) + devices * (40 << 10))
    shape = pltpu.VMEM
    result = jax.ShapeDtypeStruct

    def near(*arrays):
        return [pltpu.with_memory_space_constraint(array, pltpu.VMEM) for array in arrays]

    call = functools.partial(pl.pallas_call, compiler_params=params)
    place = lax.axis_index("grp").astype(jnp.int32)[None]

    row_shape = shape((cols, own), F32)
    message, own_points, own_right = call(
        pack_kernel,
        out_shape=(
            shape((peers, feats + 2 * cols, own), BF16), shape((feats, own), BF16), row_shape,
        ),
        in_specs=_hbm(2),
        out_specs=tuple(_vmem(3)),
        scratch_shapes=[pltpu.SemaphoreType.DMA((2,))],
        name="pack",
    )(*[pltpu.with_memory_space_constraint(array, pltpu.HBM) for array in (points, right_side)])
    vectors = [lax.all_to_all(message, "blk" if paired else axes, 0, 0, tiled=True)]
    if paired:
        vectors.append(lax.ppermute(vectors[0], "grp", SWAP))

    tile_shape = shape((peers // pair, own, pair * own), BF16)
    kerns = []
    total = []
    for part in range(part_count):
        final_part = part + 1 == part_count
        outs = [tile_shape, row_shape]
        if final_part:
            outs.append(shape((devices, cols // 2 if paired else cols, own), F32))
        tiles, *total = call(
            functools.partial(kern_kernel, pair, part > 0),
            out_shape=tuple(outs),
            in_specs=[_smem()] + _vmem(3 if part > 0 else 2),
            out_specs=tuple(_vmem(len(outs))),
            name="kern",
        )(lengthscale, *near(own_points, vectors[part], *total))
        kerns.append(tiles)
    kernel_first, message = total
    received = [lax.all_to_all(message, axes, 0, 0, tiled=True)]
    wide_shape = shape((devices, cols, own), F32)
    dkern, slope_first, wide, norm, scalars = call(
        functools.partial(dkern_kernel, part_count, pair),
        out_shape=(
            shape((devices // pair, own, pair * own), BF16), row_shape, wide_shape, row_shape,
            shape((8, 128), F32),
        ),
        in_specs=[_smem()] * 3 + _vmem(1 + part_count),
        out_specs=tuple(_vmem(5)),
        name="dkern",
    )(lengthscale, outputscale, noise_level, *near(own_points, *vectors))
    received[0], dkern = lax.optimization_barrier((received[0], dkern))
    if paired:
        received.append(lax.ppermute(received[0], "grp", SWAP))

    message, direction, residual, applied, columns, products, turned = call(
        functools.partial(second_kernel, part_count, pair, len(received)),
        out_shape=(
            shape((devices, 2, own), F32), row_shape, row_shape, row_shape, shape((cols, 128), F32),
            wide_shape, wide_shape,
        ),
        in_specs=[_smem()] + _vmem(7 + part_count + len(received)),
        out_specs=tuple(_vmem(7)),
        name="second",
    )(
        place,
        *near(scalars, own_right, kernel_first, slope_first, dkern, wide, norm, *kerns, *received),
    )
    received = lax.all_to_all(message, axes, 0, 0, tiled=True)
    middle = call(
        functools.partial(middle_kernel, part_count),
        out_shape=shape((cols, 128), F32),
        in_specs=_vmem(3),
        out_specs=_vmem(1)[0],
        name="middle",
    )(*near(wide, products, turned))

    solution, final, gradient = call(
        functools.partial(last_kernel, part_count, float(own * devices)),
        out_shape=(result((cols, own), F32), result((cols, own), F32), result((3,), F32)),
        in_specs=[_smem()] + _vmem(11),
        out_specs=tuple(_hbm(2) + [_smem()]),
        scratch_shapes=[
            pltpu.VMEM((cols, own), F32),
            pltpu.VMEM((cols, own), F32),
            pltpu.SemaphoreType.DMA((2,)),
        ],
        name="last",
    )(
        place,
        *near(scalars, own_right, direction, residual, applied, columns, middle, wide, products, turned, received),
    )
    return solution, final, gradient


def solution(mesh):
    whole = P(None, ("blk", "grp"))
    return jax.shard_map(
        functools.partial(local, dict(mesh.shape)),
        mesh=mesh,
        in_specs=(whole, whole, P(), P(), P()),
        out_specs=(whole, whole, P()),
        check_vma=False,
    )
```

time: 53.4 us -> 50.7 us (0.949)
  blocking collectives: 30.2 us -> 20.8 us
  waiting for transfers between devices: 8.13 us -> 13.1 us
  starting transfers between devices: 2.59 us -> 5.33 us
  local copies, waits for them, and re-layouts: 1.42 us -> 0 us
    all_to_all x2 -> x1, blocking collectives: 30.2 us -> 20.8 us  [local(): lax.all_to_all(message, 'blk' if paired else axes, 0, 0, tiled=True)]
    all_to_all x1 -> x2, waiting for transfers between devices: 7.06 us -> 11.7 us  [the longest x1 7.02 us: local(): received = lax.all_to_all(message, axes, 0, 0, tiled=True)]
    all_to_all x1 -> x2, starting transfers between devices: 2.59 us -> 5.11 us  [the longest x1 2.59 us: local(): received = [lax.all_to_all(message, axes, 0, 0, tiled=True)]]
    unnamed x8 -> x0, local copies, waits for them, and re-layouts: 1.42 us -> none
    pallas_call x5 -> x7, Pallas kernels: 7.98 us -> 8.44 us  [the longest x2 2.26 us: local(): call(functools.partial(kern_kernel, pair, part > 0), out_shape=tuple(outs...]
    ppermute x1 -> x2, waiting for transfers between devices: 1.07 us -> 1.43 us  [the longest x1 1.13 us: local(): received.append(lax.ppermute(received[0], 'grp', SWAP))]
  transfers between devices with their start and end apart: 2 -> 4, of which waited for: 2 -> 4; matrix products, arithmetic and copies ran while one was open for 0% -> 0% of each run, Pallas kernels for 4% -> 6%
where the time goes in v3:
time: 50.7 us; the launch traced here: 50.3 us
  blocking collectives  20.8 us (41%)
  waiting for transfers between devices  13.1 us (26%)
  Pallas kernels  8.44 us (17%)
  starting transfers between devices  5.33 us (11%)
  between operations  2.61 us (5%)
    all_to_all x1, blocking collectives, local(): lax.all_to_all(message, 'blk' if paired else axes, 0, 0, tiled=True)  20.8 us
    all_to_all x1, waiting for transfers between devices, local(): received = lax.all_to_all(message, axes, 0, 0, tiled=True)  7.02 us
    all_to_all x1, waiting for transfers between devices, local(): received = [lax.all_to_all(message, axes, 0, 0, tiled=True)]  4.7 us
    all_to_all x1, starting transfers between devices, local(): received = [lax.all_to_all(message, axes, 0, 0, tiled=True)]  2.59 us
    all_to_all x1, starting transfers between devices, local(): received = lax.all_to_all(message, axes, 0, 0, tiled=True)  2.52 us
    pallas_call x2, Pallas kernels, local(): call(functools.partial(kern_kernel, pair, part > 0), out_shape=tuple(outs...  2.26 us
    pallas_call x1, Pallas kernels, local(): call(functools.partial(dkern_kernel, part_count, pair), out_shape=(shape(...  2.21 us
    pallas_call x1, Pallas kernels, local(): call(functools.partial(second_kernel, part_count, pair, len(received)), o...  1.63 us
  transfers between devices with their start and end apart: 4, of which 4 were waited for; matrix products, arithmetic and copies ran while one was open for 0% of the time, Pallas kernels for 6%

profile of v3, /device:TPU:0, one launch (start us, length us, event | category | flops | bytes accessed | tf_op | source)
XLA Modules:
  0.0 50.3 jit_solution(10567212124924949741)
XLA Ops:
  0.6 0.8 %pack.1 = (bf16[16,96,128]{2,1,0:T(8,128)(2,1)S(1)}, bf16[64,128]{1,0:T(8,128)(2,1)S(1)}, f32[16,128]{1,0:T(8,128)S(1)}) custom-call(bf16[64,128]{1,0:T(8,128)(2,1)} %points_hbm.1, f32[16,128]{1,0:T(8,128)} %right_hbm.1), custom_call_target="tpu_custom_call" | custom-call | tf_op jit(solution)/shard_map/pack/pallas_call | solution.py:397
  1.4 20.8 %all_to_all.15.refs_0_.part_ref = bf16[16,96,128]{2,1,0:T(8,128)(2,1)S(1)} all-to-all(bf16[16,96,128]{2,1,0:T(8,128)(2,1)S(1)} %get-tuple-element.26), channel_id=1, replica_groups=mesh['blk'=16,'grp'=2] {'blk'}, dimensions={0} | all-to-all | bytes 786432 | tf_op jit(solution)/shard_map/all_to_all | solution.py:407
  22.2 0.0 collective-permute-start
  22.8 0.8 %kern.2 = (bf16[8,128,256]{2,1,0:T(8,128)(2,1)S(1)}, f32[16,128]{1,0:T(8,128)S(1)}) custom-call(f32[1]{0:T(128)S(6)} %copy.8.length_ref, bf16[64,128]{1,0:T(8,128)(2,1)S(1)} %get-tuple-element.25.points_ref, bf16[16,96,128]{2,1,0:T(8,128)(2,1)S(1)} %all_to_all.15.refs_0_.part_ref), custom_call_target="tpu_custom_call" | custom-call | tf_op jit(solution)/shard_map/kern/pallas_call | solution.py:419
  23.6 0.3 collective-permute-done.refs_1_.part_ref
  23.9 1.5 %kern.3 = (bf16[8,128,256]{2,1,0:T(8,128)(2,1)S(1)}, f32[16,128]{1,0:T(8,128)S(1)}, f32[32,8,128]{2,1,0:T(8,128)}) custom-call(f32[1]{0:T(128)S(6)} %copy.8.length_ref, bf16[64,128]{1,0:T(8,128)(2,1)S(1)} %get-tuple-element.25.points_ref, bf16[16,96,128]{2,1,0:T(8,128)(2,1)S(1)} %collective-permute-done.refs_1_.part_ref, f32[16,128]{1,0:T(8,128)S(1)} %get-tuple-element.29.refs_0_), custom_call_target="tpu_custom_call" | custom-call | tf_op jit(solution)/shard_map/kern/pallas_call | solution.py:419
  25.4 2.6 %all-to-all-start.1 = ((f32[32,8,128]{2,1,0:T(8,128)}), f32[32,8,128]{2,1,0:T(8,128)S(1)}, u32[]{:S(2)}, u32[]{:S(2)}) async-start(f32[32,8,128]{2,1,0:T(8,128)} %get-tuple-element.32), calls=%async_computation.1 | async-start | bytes 262144 | tf_op jit(solution)/shard_map/all_to_all | solution.py:428
  29.3 2.2 %dkern.1 = (bf16[16,128,256]{2,1,0:T(8,128)(2,1)S(1)}, f32[16,128]{1,0:T(8,128)S(1)}, f32[32,16,128]{2,1,0:T(8,128)S(1)}, f32[16,128]{1,0:T(8,128)S(1)}, f32[8,128]{1,0:T(8,128)S(1)}) custom-call(f32[1]{0:T(128)S(6)} %copy.8.length_ref, f32[1]{0:T(128)S(6)} %copy.9.amplitude_ref, f32[1]{0:T(128)S(6)} %copy.10.jitter_ref, ...), custom_call_target="tpu_custom_call" | custom-call | tf_op jit(solution)/shard_map/dkern/pallas_call | solution.py:430
  31.5 4.7 %all-to-all-done.1.refs_2_ = f32[32,8,128]{2,1,0:T(8,128)S(1)} async-done(((f32[32,8,128]{2,1,0:T(8,128)}), f32[32,8,128]{2,1,0:T(8,128)S(1)}, u32[]{:S(2)}, u32[]{:S(2)}) %all-to-all-start.1) | async-done | bytes 131104 | tf_op jit(solution)/shard_map/all_to_all | solution.py:428
  36.2 0.2 collective-permute-start.1
  36.4 1.1 %collective-permute-done.1.refs_3_ = f32[32,8,128]{2,1,0:T(8,128)S(1)} collective-permute-done((f32[32,8,128]{2,1,0:T(8,128)S(1)}, f32[32,8,128]{2,1,0:T(8,128)S(1)}, u32[]{:S(2)}, u32[]{:S(2)}) %collective-permute-start.1) | collective-permute-done | bytes 131104 | tf_op jit(solution)/shard_map/ppermute | solution.py:442
  37.5 1.6 %second.1 = (f32[32,2,128]{2,1,0:T(2,128)}, f32[16,128]{1,0:T(8,128)S(1)}, f32[16,128]{1,0:T(8,128)S(1)}, f32[16,128]{1,0:T(8,128)S(1)}, f32[16,128]{1,0:T(8,128...) custom-call(s32[1]{0:T(128)} %bitcast.place_ref, f32[8,128]{1,0:T(8,128)S(1)} %get-tuple-element.27.scalars_ref, ...), custom_call_target="tpu_custom_call" | custom-call | tf_op jit(solution)/shard_map/second/pallas_call | solution.py:444
  39.2 2.5 %all-to-all-start.2 = ((f32[32,2,128]{2,1,0:T(2,128)}), f32[32,2,128]{2,1,0:T(2,128)S(1)}, u32[]{:S(2)}, u32[]{:S(2)}) async-start(f32[32,2,128]{2,1,0:T(2,128)} %get-tuple-element.46), calls=%async_computation.2 | async-start | bytes 65536 | tf_op jit(solution)/shard_map/all_to_all | solution.py:457
  41.7 0.2 middle.1.middle_ref
  41.9 7.0 %all-to-all-done.2.received_ref = f32[32,2,128]{2,1,0:T(2,128)S(1)} async-done(((f32[32,2,128]{2,1,0:T(2,128)}), f32[32,2,128]{2,1,0:T(2,128)S(1)}, u32[]{:S(2)}, u32[]{:S(2)}) %all-to-all-start.2) | async-done | bytes 32800 | tf_op jit(solution)/shard_map/all_to_all | solution.py:457
  49.0 1.3 %last.1 = (f32[16,128]{1,0:T(8,128)}, f32[16,128]{1,0:T(8,128)}, f32[3]{0:T(128)}) custom-call(s32[1]{0:T(128)} %bitcast.place_ref, f32[8,128]{1,0:T(8,128)S(1)} %get-tuple-element.27.scalars_ref, f32[16,128]{1,0:T(8,128)S(1)} %get-tuple-element.28.right_ref, f32[16,128]{1,0:T(8,128)S(1)} %get-tuple-element.40.direction_ref, ...), custom_call_target="tpu_custom_call" | custom-call | tf_op jit(solution)/shard_map/last/pallas_call | solution.py:466
Async XLA Ops:
  22.2 1.7 %collective-permute-start = (bf16[16,96,128]{2,1,0:T(8,128)(2,1)S(1)}, bf16[16,96,128]{2,1,0:T(8,128)(2,1)S(1)}, u32[]{:S(2)}, u32[]{:S(2)}) collective-permute-start(bf16[16,96,128]{2,1,0:T(8,128)(2,1)S(1)} %all_to_all.15.refs_0_.part_ref), channel_id=1, source_target_pairs={{0,1},{1,0},{2,3},{3,2},{4,5},{5,4},{6,7},{7,6},{8,9},{9,8},{10,11... | collective-permute-start | bytes 1179656 | tf_op jit(solution)/shard_map/ppermute | solution.py:409
  25.4 10.8 %all-to-all-start.1 = ((f32[32,8,128]{2,1,0:T(8,128)}), f32[32,8,128]{2,1,0:T(8,128)S(1)}, u32[]{:S(2)}, u32[]{:S(2)}) async-start(f32[32,8,128]{2,1,0:T(8,128)} %get-tuple-element.32), calls=%async_computation.1 | async-start | bytes 262144 | tf_op jit(solution)/shard_map/all_to_all | solution.py:428
  36.2 1.3 %collective-permute-start.1 = (f32[32,8,128]{2,1,0:T(8,128)S(1)}, f32[32,8,128]{2,1,0:T(8,128)S(1)}, u32[]{:S(2)}, u32[]{:S(2)}) collective-permute-start(f32[32,8,128]{2,1,0:T(8,128)S(1)} %all-to-all-done.1.refs_2_), channel_id=1, source_target_pairs={{0,1},{1,0},{2,3},{3,2},{4,5},{5,4},{6,7},{7,6},{8,9},{9,8},{10,11... | collective-permute-start | bytes 393224 | tf_op jit(solution)/shard_map/ppermute | solution.py:442
  39.2 9.8 %all-to-all-start.2 = ((f32[32,2,128]{2,1,0:T(2,128)}), f32[32,2,128]{2,1,0:T(2,128)S(1)}, u32[]{:S(2)}, u32[]{:S(2)}) async-start(f32[32,2,128]{2,1,0:T(2,128)} %get-tuple-element.46), calls=%async_computation.2 | async-start | bytes 65536 | tf_op jit(solution)/shard_map/all_to_all | solution.py:457

commit v4 on v3

--- a/solution.py
+++ b/solution.py
@@ -156,17 +156,10 @@
     norm_ref[...] = jnp.broadcast_to(lane_sum(functools.reduce(jnp.add, norms)), norm_ref.shape)
 
 
-def to_lanes(column, slot):
-    cols = column.shape[0]
+def from_lanes(row, first, cols):
     lanes = lax.broadcasted_iota(jnp.int32, (cols, 128), 1)
     rows = lax.broadcasted_iota(jnp.int32, (cols, 128), 0)
-    return jnp.where(lanes == rows + slot * cols, jnp.broadcast_to(column, (cols, 128)), 0.0)
-
-
-def from_lanes(row, slot, cols):
-    lanes = lax.broadcasted_iota(jnp.int32, (cols, 128), 1)
-    rows = lax.broadcasted_iota(jnp.int32, (cols, 128), 0)
-    picked = jnp.where(lanes == rows + slot * cols, jnp.broadcast_to(row, (cols, 128)), 0.0)
+    picked = jnp.where(lanes == rows + first, jnp.broadcast_to(row, (cols, 128)), 0.0)
     return lane_sum(picked)
 
 
@@ -257,56 +250,32 @@
     direction_ref[...] = direction
     residual_ref[...] = residual
     applied_ref[...] = applied
-    columns_ref[...] = into_columns([step, norm_next, norm], cols)
+    columns_ref[...] = into_columns([step, norm_next, norm, turn], cols)
 
     low = right - right.astype(BF16).astype(F32)
     low_direction = direction - direction.astype(BF16).astype(F32)
     slope = slope_ref[...]
+    lanes = lax.broadcasted_iota(jnp.int32, (cols, 128), 1)
+    rows = lax.broadcasted_iota(jnp.int32, (cols, 128), 0)
     packed = jnp.zeros((cols, 128), F32)
     for slot, values in enumerate([
-        direction * applied,
-        low * total,
-        right * slope,
-        right * slopes,
-        direction * slope,
-        direction * slopes,
-        low_direction * total,
+        direction * applied, low * total, low * kernel_ref[...], right * slope, right * slopes,
     ]):
-        packed = packed + to_lanes(lane_sum(values), slot)
+        packed = jnp.where(lanes == rows + slot * cols, lane_sum(values), packed)
+    rows = jnp.where(rows == 0, 5 * cols, 128)
+    for slot, values in enumerate([
+        direction * slope, direction * slopes, low_direction * kernel_ref[...], low_direction * total,
+    ]):
+        packed = jnp.where(lanes == rows + slot, lane_sum(values), packed)
     packed = jnp.sum(packed, axis=0, keepdims=True)
     for peer in range(message_ref.shape[0]):
         message_ref[peer, 0:1, :] = packed
         message_ref[peer, 1:2, :] = total[0:1, :]
 
 
-def middle_kernel(part_count, wide_ref, products_ref, turned_ref, out_ref):
-    blocks, cols, own = wide_ref.shape
-    count = blocks // part_count
-    zero = jnp.zeros((cols, own), F32)
-    sums = []
-    for part in range(part_count):
-        def one_block(block, carried, part=part):
-            block = part * count + block
-            right = wide_ref[block]
-            direction = turned_ref[block]
-            product = products_ref[block]
-            low = right - right.astype(BF16).astype(F32)
-            low_direction = direction - direction.astype(BF16).astype(F32)
-            return (
-                carried[0] + low * product,
-                carried[1] + low_direction * product,
-                carried[2] + right * direction,
-                carried[3] + direction * direction,
-            )
-
-        sums.append(lax.fori_loop(0, count, one_block, (zero,) * 4, unroll=unrolled(count, 4)))
-    sums = [lane_sum(functools.reduce(jnp.add, parts)) for parts in zip(*sums)]
-    out_ref[...] = into_columns(sums, cols)
-
-
 def last_kernel(
     part_count, points_total, place_ref, scalars_ref, right_ref, direction_ref, residual_ref,
-    applied_ref, columns_ref, middle_ref, wide_ref, products_ref, turned_ref, received_ref,
+    applied_ref, columns_ref, wide_ref, products_ref, turned_ref, received_ref,
     solution_hbm, final_hbm, gradient_ref, solution_ref, final_ref, sems
 ):
     cols, own = right_ref.shape
@@ -332,10 +301,15 @@
     for copy in copies:
         copy.start()
 
-    low_next, right_slope, right_slope_next, slope_cross, slope_square, low_square = [
-        from_lanes(sums, slot, cols) for slot in range(1, 7)
+    low_next, low_first, right_slope, right_slope_next = [
+        from_lanes(sums, slot * cols, cols) for slot in range(1, 5)
     ]
-    low_first, low_second, dots, squares = [middle_ref[:, slot : slot + 1] for slot in range(4)]
+    slope_cross, slope_square, low_second, low_square = [
+        sums[:, 5 * cols + slot : 5 * cols + slot + 1] for slot in range(4)
+    ]
+    turn = columns_ref[:, 3:4]
+    dots = turn * norm
+    squares = norm_next + turn * dots
     count = wide_ref.shape[0] // part_count
     zero = jnp.zeros((cols, own), F32)
     row_zero = jnp.zeros((1, own), F32)
@@ -354,16 +328,18 @@
         sums.append(lax.fori_loop(0, count, one_block, (zero, row_zero), unroll=unrolled(count, 8)))
     whole, first_row = [functools.reduce(jnp.add, parts) for parts in zip(*sums)]
     right_kernel = lane_sum(whole) + step * low_first + step_next * low_next
-    direction_kernel = lane_sum(first_row) + (step * low_second + step_next * low_square)[0:1, :]
+    first_step, second_step = step[0:1], step_next[0:1]
+    direction_kernel = lane_sum(first_row) + first_step * low_second + second_step * low_square
+    direction_slope = first_step * slope_cross + second_step * slope_square
     is_first = lax.broadcasted_iota(jnp.int32, (cols, 1), 0) == 0
     weight = jnp.where(is_first, 1.0, -1.0 / (cols - 1))
     for slot, (right_form, direction_form) in enumerate((
         (
             amplitude[:, 0:1] * (step * right_slope + step_next * right_slope_next),
-            amplitude[:, 0:1] * (step * slope_cross + step_next * slope_square),
+            amplitude[:, 0:1] * direction_slope,
         ),
-        (right_kernel, jnp.broadcast_to(direction_kernel, (cols, 1))),
-        (step * norm + step_next * dots, step * dots + step_next * squares),
+        (right_kernel, direction_kernel),
+        (step * norm + step_next * dots, (step * dots + step_next * squares)[0:1]),
     )):
         form = jnp.where(is_first, step * right_form + step_next * direction_form, right_form)
         gradient_ref[slot] = jnp.sum(weight * form) * (0.5 / points_total)
@@ -455,18 +431,11 @@
         *near(scalars, own_right, kernel_first, slope_first, dkern, wide, norm, *kerns, *received),
     )
     received = lax.all_to_all(message, axes, 0, 0, tiled=True)
-    middle = call(
-        functools.partial(middle_kernel, part_count),
-        out_shape=shape((cols, 128), F32),
-        in_specs=_vmem(3),
-        out_specs=_vmem(1)[0],
-        name="middle",
-    )(*near(wide, products, turned))
 
     solution, final, gradient = call(
         functools.partial(last_kernel, part_count, float(own * devices)),
         out_shape=(result((cols, own), F32), result((cols, own), F32), result((3,), F32)),
-        in_specs=[_smem()] + _vmem(11),
+        in_specs=[_smem()] + _vmem(10),
         out_specs=tuple(_hbm(2) + [_smem()]),
         scratch_shapes=[
             pltpu.VMEM((cols, own), F32),
@@ -476,7 +445,7 @@
         name="last",
     )(
         place,
-        *near(scalars, own_right, direction, residual, applied, columns, middle, wide, products, turned, received),
+        *near(scalars, own_right, direction, residual, applied, columns, wide, products, turned, received),
     )
     return solution, final, gradient
 

time: 50.7 us -> 49.3 us (0.972)
  blocking collectives: 20.8 us -> 29.8 us
  waiting for transfers between devices: 13.1 us -> 6.12 us
  starting transfers between devices: 5.33 us -> 2.81 us
  Pallas kernels: 8.44 us -> 7.59 us
    all_to_all x0 -> x1, blocking collectives: none -> 9.02 us  [local(): received = lax.all_to_all(message, axes, 0, 0, tiled=True)]
    all_to_all x1 -> x0, waiting for transfers between devices: 7.02 us -> none  [local(): received = lax.all_to_all(message, axes, 0, 0, tiled=True)]
    all_to_all x1 -> x0, starting transfers between devices: 2.52 us -> none  [local(): received = lax.all_to_all(message, axes, 0, 0, tiled=True)]
    pallas_call x1, Pallas kernels: 1.63 us -> 1 us  [local(): call(functools.partial(second_kernel, part_count, pair, len(received)), o...]
  transfers between devices with their start and end apart: 4 -> 3, of which waited for: 4 -> 3; matrix products, arithmetic and copies ran while one was open for 0% -> 0% of each run, Pallas kernels for 6% -> 6%
where the time goes in v4:
time: 49.3 us; the launch traced here: 48.9 us
  blocking collectives  29.8 us (60%)
  Pallas kernels  7.59 us (15%)
  waiting for transfers between devices  6.12 us (12%)
  starting transfers between devices  2.81 us (6%)
  between operations  2.61 us (5%)
    all_to_all x1, blocking collectives, local(): lax.all_to_all(message, 'blk' if paired else axes, 0, 0, tiled=True)  20.8 us
    all_to_all x1, blocking collectives, local(): received = lax.all_to_all(message, axes, 0, 0, tiled=True)  9.02 us
    all_to_all x1, waiting for transfers between devices, local(): received = [lax.all_to_all(message, axes, 0, 0, tiled=True)]  4.7 us
    all_to_all x1, starting transfers between devices, local(): received = [lax.all_to_all(message, axes, 0, 0, tiled=True)]  2.59 us
    pallas_call x2, Pallas kernels, local(): call(functools.partial(kern_kernel, pair, part > 0), out_shape=tuple(outs...  2.27 us
    pallas_call x1, Pallas kernels, local(): call(functools.partial(dkern_kernel, part_count, pair), out_shape=(shape(...  2.21 us
    pallas_call x1, Pallas kernels, local(): call(functools.partial(last_kernel, part_count, float(own * devices)), ou...  1.32 us
    ppermute x1, waiting for transfers between devices, local(): received.append(lax.ppermute(received[0], 'grp', SWAP))  1.13 us
  transfers between devices with their start and end apart: 3, of which 3 were waited for; matrix products, arithmetic and copies ran while one was open for 0% of the time, Pallas kernels for 6%

profile of v4, /device:TPU:0, one launch (start us, length us, event | category | flops | bytes accessed | tf_op | source)
XLA Modules:
  0.0 48.9 jit_solution(13147436292488577088)
XLA Ops:
  0.6 0.8 %pack.1 = (bf16[16,96,128]{2,1,0:T(8,128)(2,1)S(1)}, bf16[64,128]{1,0:T(8,128)(2,1)S(1)}, f32[16,128]{1,0:T(8,128)S(1)}) custom-call(bf16[64,128]{1,0:T(8,128)(2,1)} %points_hbm.1, f32[16,128]{1,0:T(8,128)} %right_hbm.1), custom_call_target="tpu_custom_call" | custom-call | tf_op jit(solution)/shard_map/pack/pallas_call | solution.py:373
  1.4 20.8 %all_to_all.15.refs_0_.part_ref = bf16[16,96,128]{2,1,0:T(8,128)(2,1)S(1)} all-to-all(bf16[16,96,128]{2,1,0:T(8,128)(2,1)S(1)} %get-tuple-element.26), channel_id=1, replica_groups=mesh['blk'=16,'grp'=2] {'blk'}, dimensions={0} | all-to-all | bytes 786432 | tf_op jit(solution)/shard_map/all_to_all | solution.py:383
  22.2 0.0 collective-permute-start
  22.8 0.8 %kern.2 = (bf16[8,128,256]{2,1,0:T(8,128)(2,1)S(1)}, f32[16,128]{1,0:T(8,128)S(1)}) custom-call(f32[1]{0:T(128)S(6)} %copy.8.length_ref, bf16[64,128]{1,0:T(8,128)(2,1)S(1)} %get-tuple-element.25.points_ref, bf16[16,96,128]{2,1,0:T(8,128)(2,1)S(1)} %all_to_all.15.refs_0_.part_ref), custom_call_target="tpu_custom_call" | custom-call | tf_op jit(solution)/shard_map/kern/pallas_call | solution.py:395
  23.6 0.3 collective-permute-done.refs_1_.part_ref
  23.9 1.5 %kern.3 = (bf16[8,128,256]{2,1,0:T(8,128)(2,1)S(1)}, f32[16,128]{1,0:T(8,128)S(1)}, f32[32,8,128]{2,1,0:T(8,128)}) custom-call(f32[1]{0:T(128)S(6)} %copy.8.length_ref, bf16[64,128]{1,0:T(8,128)(2,1)S(1)} %get-tuple-element.25.points_ref, bf16[16,96,128]{2,1,0:T(8,128)(2,1)S(1)} %collective-permute-done.refs_1_.part_ref, f32[16,128]{1,0:T(8,128)S(1)} %get-tuple-element.29.refs_0_), custom_call_target="tpu_custom_call" | custom-call | tf_op jit(solution)/shard_map/kern/pallas_call | solution.py:395
  25.4 2.6 %all-to-all-start.1 = ((f32[32,8,128]{2,1,0:T(8,128)}), f32[32,8,128]{2,1,0:T(8,128)S(1)}, u32[]{:S(2)}, u32[]{:S(2)}) async-start(f32[32,8,128]{2,1,0:T(8,128)} %get-tuple-element.32), calls=%async_computation.1 | async-start | bytes 262144 | tf_op jit(solution)/shard_map/all_to_all | solution.py:404
  29.3 2.2 %dkern.1 = (bf16[16,128,256]{2,1,0:T(8,128)(2,1)S(1)}, f32[16,128]{1,0:T(8,128)S(1)}, f32[32,16,128]{2,1,0:T(8,128)S(1)}, f32[16,128]{1,0:T(8,128)S(1)}, f32[8,128]{1,0:T(8,128)S(1)}) custom-call(f32[1]{0:T(128)S(6)} %copy.8.length_ref, f32[1]{0:T(128)S(6)} %copy.9.amplitude_ref, f32[1]{0:T(128)S(6)} %copy.10.jitter_ref, ...), custom_call_target="tpu_custom_call" | custom-call | tf_op jit(solution)/shard_map/dkern/pallas_call | solution.py:406
  31.5 4.7 %all-to-all-done.1.refs_2_ = f32[32,8,128]{2,1,0:T(8,128)S(1)} async-done(((f32[32,8,128]{2,1,0:T(8,128)}), f32[32,8,128]{2,1,0:T(8,128)S(1)}, u32[]{:S(2)}, u32[]{:S(2)}) %all-to-all-start.1) | async-done | bytes 131104 | tf_op jit(solution)/shard_map/all_to_all | solution.py:404
  36.2 0.2 collective-permute-start.1
  36.4 1.1 %collective-permute-done.1.refs_3_ = f32[32,8,128]{2,1,0:T(8,128)S(1)} collective-permute-done((f32[32,8,128]{2,1,0:T(8,128)S(1)}, f32[32,8,128]{2,1,0:T(8,128)S(1)}, u32[]{:S(2)}, u32[]{:S(2)}) %collective-permute-start.1) | collective-permute-done | bytes 131104 | tf_op jit(solution)/shard_map/ppermute | solution.py:418
  37.6 1.0 %second.1 = (f32[32,2,128]{2,1,0:T(2,128)S(1)}, f32[16,128]{1,0:T(8,128)S(1)}, f32[16,128]{1,0:T(8,128)S(1)}, f32[16,128]{1,0:T(8,128)S(1)}, f32[16,128]{1,0:T(8...) custom-call(s32[1]{0:T(128)} %bitcast.place_ref, f32[8,128]{1,0:T(8,128)S(1)} %get-tuple-element.27.scalars_ref, ...), custom_call_target="tpu_custom_call" | custom-call | tf_op jit(solution)/shard_map/second/pallas_call | solution.py:420
  38.6 9.0 %all_to_all.16.received_ref = f32[32,2,128]{2,1,0:T(2,128)S(1)} all-to-all(f32[32,2,128]{2,1,0:T(2,128)S(1)} %get-tuple-element.46), channel_id=1, replica_groups=mesh['blk'=16,'grp'=2] {'blk','grp'}, dimensions={0} | all-to-all | bytes 65536 | tf_op jit(solution)/shard_map/all_to_all | solution.py:433
  47.6 1.3 %last.1 = (f32[16,128]{1,0:T(8,128)}, f32[16,128]{1,0:T(8,128)}, f32[3]{0:T(128)}) custom-call(s32[1]{0:T(128)} %bitcast.place_ref, f32[8,128]{1,0:T(8,128)S(1)} %get-tuple-element.27.scalars_ref, f32[16,128]{1,0:T(8,128)S(1)} %get-tuple-element.28.right_ref, f32[16,128]{1,0:T(8,128)S(1)} %get-tuple-element.40.direction_ref, ...), custom_call_target="tpu_custom_call" | custom-call | tf_op jit(solution)/shard_map/last/pallas_call | solution.py:435
Async XLA Ops:
  22.2 1.7 %collective-permute-start = (bf16[16,96,128]{2,1,0:T(8,128)(2,1)S(1)}, bf16[16,96,128]{2,1,0:T(8,128)(2,1)S(1)}, u32[]{:S(2)}, u32[]{:S(2)}) collective-permute-start(bf16[16,96,128]{2,1,0:T(8,128)(2,1)S(1)} %all_to_all.15.refs_0_.part_ref), channel_id=1, source_target_pairs={{0,1},{1,0},{2,3},{3,2},{4,5},{5,4},{6,7},{7,6},{8,9},{9,8},{10,11... | collective-permute-start | bytes 1179656 | tf_op jit(solution)/shard_map/ppermute | solution.py:385
  25.4 10.8 %all-to-all-start.1 = ((f32[32,8,128]{2,1,0:T(8,128)}), f32[32,8,128]{2,1,0:T(8,128)S(1)}, u32[]{:S(2)}, u32[]{:S(2)}) async-start(f32[32,8,128]{2,1,0:T(8,128)} %get-tuple-element.32), calls=%async_computation.1 | async-start | bytes 262144 | tf_op jit(solution)/shard_map/all_to_all | solution.py:404
  36.2 1.3 %collective-permute-start.1 = (f32[32,8,128]{2,1,0:T(8,128)S(1)}, f32[32,8,128]{2,1,0:T(8,128)S(1)}, u32[]{:S(2)}, u32[]{:S(2)}) collective-permute-start(f32[32,8,128]{2,1,0:T(8,128)S(1)} %all-to-all-done.1.refs_2_), channel_id=1, source_target_pairs={{0,1},{1,0},{2,3},{3,2},{4,5},{5,4},{6,7},{7,6},{8,9},{9,8},{10,11... | collective-permute-start | bytes 393224 | tf_op jit(solution)/shard_map/ppermute | solution.py:418

commit v5 on v4

v5 whole, which is shorter than its diff:
```python
import functools
import math

import jax
import jax.numpy as jnp
from jax import lax
from jax.experimental import pallas as pl
from jax.experimental.pallas import tpu as pltpu
from jax.sharding import PartitionSpec as P

F32 = jnp.float32
BF16 = jnp.bfloat16
LOG2E = math.log2(math.e)
TINY = 1e-36
NT = (((1,), (1,)), ((), ()))


def _vmem(count):
    return [pl.BlockSpec(memory_space=pltpu.VMEM) for _ in range(count)]


def _smem():
    return pl.BlockSpec(memory_space=pltpu.SMEM)


def _hbm(count):
    return [pl.BlockSpec(memory_space=pltpu.HBM) for _ in range(count)]


def lane_sum(values):
    return jnp.sum(values, axis=1, keepdims=True)


def unrolled(count, most):
    return max(divisor for divisor in range(1, most + 1) if count % divisor == 0)


def pack_kernel(points_hbm, right_hbm, out_ref, points_ref, right_ref, sems):
    feats = points_ref.shape[0]
    cols = right_ref.shape[0]
    copies = [
        pltpu.make_async_copy(right_hbm, right_ref, sems.at[0]),
        pltpu.make_async_copy(points_hbm, points_ref, sems.at[1]),
    ]
    for copy in copies:
        copy.start()
    copies[0].wait()
    right = right_ref[...]
    high = right.astype(BF16)
    out_ref[feats : feats + cols, :] = high
    out_ref[feats + cols : feats + 2 * cols, :] = (right - high.astype(F32)).astype(BF16)
    copies[1].wait()
    out_ref[0:feats, :] = points_ref[...]


def fan_kernel(length_ref, amplitude_ref, jitter_ref, *refs):
    *shards, out_ref, scalars_ref = refs
    for slot, scalar in enumerate((length_ref, amplitude_ref, jitter_ref)):
        scalars_ref[slot : slot + 1, :] = jnp.full((1, 128), scalar[0], F32)
    shards = [shard[...] for shard in shards]
    for peer in range(out_ref.shape[0]):
        for side, shard in enumerate(shards):
            out_ref[peer, side] = shard


def source_of(block_ref, core_ref, paired, steps, part, step, side):
    if not paired:
        return step * 2 + side
    core = core_ref[0] if part == 0 else 1 - core_ref[0]
    first = jnp.where((block_ref[0] < steps) == (side == 0), 0, steps)
    return (first + step) * 2 + core


def joined(sums):
    return functools.reduce(jnp.add, [functools.reduce(jnp.add, sides) for sides in sums])


class Distances:
    def __init__(self, scalars_ref, points_ref):
        scale = scalars_ref[0:1, :]
        self.scale = scale
        self.factor = (5.0 * LOG2E * LOG2E) / (scale * scale)
        own = points_ref.shape[1]
        points = points_ref[...].astype(F32).T
        squares = jnp.sum(points * points, axis=1, keepdims=True) * self.factor
        self.squares = jnp.broadcast_to(squares, (own, own))
        self.points = (-2.0 * points).astype(BF16)

    def __call__(self, points):
        wide = points.astype(F32)
        squares = jnp.sum(wide * wide, axis=0, keepdims=True) * self.factor
        inner = jnp.dot(self.points, points, preferred_element_type=F32)
        reduced = jnp.maximum((self.squares + squares) + inner * self.factor, TINY)
        return reduced, reduced * lax.rsqrt(reduced)


def kern_tile(reduced, root):
    shifted = root + 1.5 * LOG2E
    return (shifted * shifted + 0.75 * LOG2E * LOG2E) * jnp.exp2(-math.log2(3.0 * LOG2E * LOG2E) - root)


def kern_kernel(has_before, scalars_ref, points_ref, part_ref, *refs):
    before = refs[0][...] if has_before else None
    tiles_ref, *outs = refs[1 if has_before else 0 :]
    feats, own = points_ref.shape
    total_ref = outs[0]
    cols = total_ref.shape[0]
    distances = Distances(scalars_ref, points_ref)
    steps, sides = part_ref.shape[:2]
    total = before if has_before else jnp.zeros((cols, own), F32)

    def one_pair(step, total):
        vectors = []
        for side in range(sides):
            tile = kern_tile(*distances(part_ref[step, side, 0:feats, :]))
            tiles_ref[step, :, pl.ds(side * own, own)] = tile.astype(BF16)
            vectors.append(part_ref[step, side, feats : feats + cols, :])
        vectors = jnp.concatenate(vectors, axis=1)
        return total + lax.dot_general(vectors, tiles_ref[step], NT, preferred_element_type=F32)

    total = lax.fori_loop(0, steps, one_pair, total, unroll=unrolled(steps, 8))
    total_ref[...] = total
    if len(outs) > 1:
        message_ref = outs[1]
        rows = message_ref.shape[1]
        for peer in range(message_ref.shape[0]):
            first = (peer * rows) % cols
            message_ref[peer] = total[first : first + rows]


def dkern_kernel(part_count, scalars_ref, points_ref, *refs):
    parts = refs[:part_count]
    tiles_ref, total_ref, wide_ref, norm_ref = refs[part_count:]
    feats, own = points_ref.shape
    cols = total_ref.shape[0]
    distances = Distances(scalars_ref, points_ref)
    slope = 1.0 / (3.0 * LOG2E * LOG2E * LOG2E * distances.scale)
    total = jnp.zeros((cols, own), F32)
    norms = []
    base = 0
    for part in parts:
        steps, sides = part.shape[:2]

        def one_pair(step, carried, part=part, base=base):
            total, norm = carried
            norm = list(norm)
            vectors = []
            for side in range(sides):
                reduced, root = distances(part[step, side, 0:feats, :])
                tile = (reduced * slope) * ((root + LOG2E) * jnp.exp2(-root))
                tiles_ref[base + step, :, pl.ds(side * own, own)] = tile.astype(BF16)
                high = part[step, side, feats : feats + cols, :]
                low = part[step, side, feats + cols : feats + 2 * cols, :]
                right = high.astype(F32) + low.astype(F32)
                wide_ref[base + step, side] = right
                norm[side] = norm[side] + right * right
                vectors.append(high)
            vectors = jnp.concatenate(vectors, axis=1)
            total = total + lax.dot_general(
                vectors, tiles_ref[base + step], NT, preferred_element_type=F32
            )
            return total, tuple(norm)

        zeros = (jnp.zeros((cols, own), F32),) * sides
        total, norm = lax.fori_loop(0, steps, one_pair, (total, zeros), unroll=unrolled(steps, 4))
        norms.append(norm)
        base += steps
    total_ref[...] = total
    norm_ref[...] = jnp.broadcast_to(lane_sum(joined(norms)), norm_ref.shape)


def from_lanes(row, first, cols):
    lanes = lax.broadcasted_iota(jnp.int32, (cols, 128), 1)
    rows = lax.broadcasted_iota(jnp.int32, (cols, 128), 0)
    picked = jnp.where(lanes == rows + first, jnp.broadcast_to(row, (cols, 128)), 0.0)
    return lane_sum(picked)


def into_columns(columns, cols):
    lanes = lax.broadcasted_iota(jnp.int32, (cols, 128), 1)
    kept = jnp.zeros((cols, 128), F32)
    for slot, column in enumerate(columns):
        kept = jnp.where(lanes == slot, jnp.broadcast_to(column, (cols, 128)), kept)
    return kept


def second_kernel(
    part_count, paired, block_ref, core_ref, scalars_ref, right_ref, kernel_ref, slope_ref, dkern_ref, wide_ref,
    norm_ref, *refs
):
    kerns = refs[:part_count]
    received = refs[part_count : 2 * part_count]
    (
        message_ref, direction_ref, residual_ref, applied_ref, columns_ref, products_ref, turned_ref,
    ) = refs[2 * part_count :]
    cols, own = right_ref.shape
    sides = wide_ref.shape[1]
    amplitude = scalars_ref[1:2, :]
    jitter = scalars_ref[2:3, :]
    low_core = core_ref[0] == 0
    zero = jnp.zeros((cols, own), F32)
    norm = norm_ref[:, 0:1]
    steps = kerns[0].shape[0]

    sums = []
    for part in range(part_count):
        def first_pass(index, carried, part=part):
            carried = [list(sums) for sums in carried]
            for side in range(sides):
                source = source_of(block_ref, core_ref, paired, steps, part, index, side)
                product = received[0][source]
                if paired:
                    other = received[1][source]
                    product = jnp.concatenate(
                        [jnp.where(low_core, product, other), jnp.where(low_core, other, product)],
                        axis=0,
                    )
                products_ref[part * steps + index, side] = product
                right = wide_ref[part * steps + index, side]
                applied = amplitude * product + jitter * right
                carried[0][side] = carried[0][side] + right * applied
                carried[1][side] = carried[1][side] + applied * applied
            return tuple(tuple(sums) for sums in carried)

        sums.append(
            lax.fori_loop(0, steps, first_pass, ((zero,) * sides,) * 2, unroll=unrolled(steps, 4))
        )
    curvature, length = [lane_sum(joined(parts)) for parts in zip(*sums)]
    step = norm / curvature
    turn = (step * step * length - norm) / norm

    sums = []
    total = zero
    slopes = zero
    for part in range(part_count):
        def second_pass(index, carried, part=part):
            total, slopes, norms = carried
            norms = list(norms)
            rounded = []
            for side in range(sides):
                right = wide_ref[part * steps + index, side]
                product = products_ref[part * steps + index, side]
                residual = right - step * (amplitude * product + jitter * right)
                direction = residual + turn * right
                turned_ref[part * steps + index, side] = direction
                norms[side] = norms[side] + residual * residual
                rounded.append(direction)
            rounded = jnp.concatenate(rounded, axis=1).astype(BF16)
            total = total + lax.dot_general(
                rounded, kerns[part][index], NT, preferred_element_type=F32
            )
            slopes = slopes + lax.dot_general(
                rounded, dkern_ref[part * steps + index], NT, preferred_element_type=F32
            )
            return total, slopes, tuple(norms)

        total, slopes, norms = lax.fori_loop(
            0, steps, second_pass, (total, slopes, (zero,) * sides), unroll=unrolled(steps, 8)
        )
        sums.append(norms)
    norm_next = lane_sum(joined(sums))

    right = right_ref[...]
    residual = right - step * (amplitude * kernel_ref[...] + jitter * right)
    direction = residual + turn * right
    applied = amplitude * total + jitter * direction
    direction_ref[...] = direction
    residual_ref[...] = residual
    applied_ref[...] = applied
    columns_ref[...] = into_columns([step, norm_next, norm, turn], cols)

    low = right - right.astype(BF16).astype(F32)
    low_direction = direction - direction.astype(BF16).astype(F32)
    slope = slope_ref[...]
    lanes = lax.broadcasted_iota(jnp.int32, (cols, 128), 1)
    rows = lax.broadcasted_iota(jnp.int32, (cols, 128), 0)
    packed = jnp.zeros((cols, 128), F32)
    for slot, values in enumerate([
        direction * applied, low * total, low * kernel_ref[...], right * slope, right * slopes,
    ]):
        packed = jnp.where(lanes == rows + slot * cols, lane_sum(values), packed)
    rows = jnp.where(rows == 0, 5 * cols, 128)
    for slot, values in enumerate([
        direction * slope, direction * slopes, low_direction * kernel_ref[...], low_direction * total,
    ]):
        packed = jnp.where(lanes == rows + slot, lane_sum(values), packed)
    packed = jnp.sum(packed, axis=0, keepdims=True)
    for peer in range(message_ref.shape[0]):
        message_ref[peer, 0:1, :] = packed
        message_ref[peer, 1:2, :] = total[0:1, :]


def last_kernel(
    part_count, paired, points_total, block_ref, core_ref, scalars_ref, right_ref, direction_ref, residual_ref,
    applied_ref, columns_ref, wide_ref, products_ref, turned_ref, received_ref,
    solution_hbm, final_hbm, gradient_ref, solution_ref, final_ref, sems
):
    cols, own = right_ref.shape
    amplitude = scalars_ref[1:2, :]
    devices = received_ref.shape[0]

    def gather_sums(device, carried):
        return carried + received_ref[device, 0:1, :]

    sums = lax.fori_loop(
        0, devices, gather_sums, jnp.zeros((1, 128), F32), unroll=unrolled(devices, 32)
    )
    step, norm_next, norm = [columns_ref[:, slot : slot + 1] for slot in range(3)]
    step_next = norm_next / from_lanes(sums, 0, cols)

    solution_ref[...] = step * right_ref[...] + step_next * direction_ref[...]
    final_ref[...] = residual_ref[...] - step_next * applied_ref[...]
    copies = [
        pltpu.make_async_copy(solution_ref, solution_hbm, sems.at[0]),
        pltpu.make_async_copy(final_ref, final_hbm, sems.at[1]),
    ]
    for copy in copies:
        copy.start()

    low_next, low_first, right_slope, right_slope_next = [
        from_lanes(sums, slot * cols, cols) for slot in range(1, 5)
    ]
    slope_cross, slope_square, low_second, low_square = [
        sums[:, 5 * cols + slot : 5 * cols + slot + 1] for slot in range(4)
    ]
    turn = columns_ref[:, 3:4]
    dots = turn * norm
    squares = norm_next + turn * dots
    steps, sides = wide_ref.shape[0] // part_count, wide_ref.shape[1]
    zero = jnp.zeros((cols, own), F32)
    row_zero = jnp.zeros((1, own), F32)
    sums = []
    for part in range(part_count):
        def one_pair(index, carried, part=part):
            carried = [list(sums) for sums in carried]
            block = part * steps + index
            for side in range(sides):
                vector = step * wide_ref[block, side] + step_next * turned_ref[block, side]
                rounded = vector.astype(BF16).astype(F32)
                source = source_of(block_ref, core_ref, paired, steps, part, index, side)
                carried[0][side] = carried[0][side] + products_ref[block, side] * rounded
                carried[1][side] = carried[1][side] + received_ref[source, 1:2, :] * rounded[0:1, :]
            return tuple(tuple(sums) for sums in carried)

        start = ((zero,) * sides, (row_zero,) * sides)
        sums.append(lax.fori_loop(0, steps, one_pair, start, unroll=unrolled(steps, 4)))
    whole, first_row = [joined(parts) for parts in zip(*sums)]
    right_kernel = lane_sum(whole) + step * low_first + step_next * low_next
    first_step, second_step = step[0:1], step_next[0:1]
    direction_kernel = lane_sum(first_row) + first_step * low_second + second_step * low_square
    direction_slope = first_step * slope_cross + second_step * slope_square
    is_first = lax.broadcasted_iota(jnp.int32, (cols, 1), 0) == 0
    weight = jnp.where(is_first, 1.0, -1.0 / (cols - 1))
    for slot, (right_form, direction_form) in enumerate((
        (
            amplitude[:, 0:1] * (step * right_slope + step_next * right_slope_next),
            amplitude[:, 0:1] * direction_slope,
        ),
        (right_kernel, direction_kernel),
        (step * norm + step_next * dots, (step * dots + step_next * squares)[0:1]),
    )):
        form = jnp.where(is_first, step * right_form + step_next * direction_form, right_form)
        gradient_ref[slot] = jnp.sum(weight * form) * (0.5 / points_total)
    for copy in copies:
        copy.wait()


SWAP = [(0, 1), (1, 0)]


def local(mesh_shape, points, right_side, lengthscale, outputscale, noise_level):
    axes = ("blk", "grp")
    feats, own = points.shape
    cols = right_side.shape[0]
    rows = feats + 2 * cols
    blocks = mesh_shape["blk"]
    devices = blocks * mesh_shape["grp"]
    paired = mesh_shape["grp"] == 2 and blocks % 2 == 0
    part_count = 2 if paired else 1
    steps = devices // (2 * part_count)
    params = pltpu.CompilerParams(vmem_limit_bytes=(4 << 20) + devices * (40 << 10))
    shape = pltpu.VMEM
    result = jax.ShapeDtypeStruct

    def near(*arrays):
        return [pltpu.with_memory_space_constraint(array, pltpu.VMEM) for array in arrays]

    call = functools.partial(pl.pallas_call, compiler_params=params)
    place = [lax.axis_index(axis).astype(jnp.int32)[None] for axis in axes]

    row_shape = shape((cols, own), F32)
    shard, own_points, own_right = call(
        pack_kernel,
        out_shape=(shape((rows, own), BF16), shape((feats, own), BF16), row_shape),
        in_specs=_hbm(2),
        out_specs=tuple(_vmem(3)),
        scratch_shapes=[pltpu.SemaphoreType.DMA((2,))],
        name="pack",
    )(*[pltpu.with_memory_space_constraint(array, pltpu.HBM) for array in (points, right_side)])
    shards = [shard]
    if paired:
        half = blocks // 2
        shards.append(lax.ppermute(shard, "blk", [(at, (at + half) % blocks) for at in range(blocks)]))
    peers = blocks // 2 if paired else devices
    message, scalars = call(
        fan_kernel,
        out_shape=(shape((peers, len(shards), rows, own), BF16), shape((8, 128), F32)),
        in_specs=[_smem()] * 3 + _vmem(len(shards)),
        out_specs=tuple(_vmem(2)),
        name="fan",
    )(lengthscale, outputscale, noise_level, *near(*shards))
    if paired:
        groups = [
            [2 * (side * half + at) + core for at in range(half)] for side in range(2) for core in range(2)
        ]
        vectors = [lax.all_to_all(message, axes, 0, 0, tiled=True, axis_index_groups=groups)]
        vectors.append(lax.ppermute(vectors[0], "grp", SWAP))
    else:
        vectors = [lax.all_to_all(message, axes, 0, 0, tiled=True).reshape(steps, 2, rows, own)]

    kerns = []
    total = []
    for part in range(part_count):
        outs = [shape((steps, own, 2 * own), BF16), row_shape]
        if part + 1 == part_count:
            outs.append(shape((devices, cols // part_count, own), F32))
        tiles, *total = call(
            functools.partial(kern_kernel, part > 0),
            out_shape=tuple(outs),
            in_specs=_vmem(4 if part > 0 else 3),
            out_specs=tuple(_vmem(len(outs))),
            name="kern",
        )(*near(scalars, own_points, vectors[part], *total))
        kerns.append(tiles)
    kernel_first, message = total
    received = [lax.all_to_all(message, axes, 0, 0, tiled=True)]
    wide_shape = shape((devices // 2, 2, cols, own), F32)
    dkern, slope_first, wide, norm = call(
        functools.partial(dkern_kernel, part_count),
        out_shape=(
            shape((devices // 2, own, 2 * own), BF16), row_shape, wide_shape, row_shape,
        ),
        in_specs=_vmem(2 + part_count),
        out_specs=tuple(_vmem(4)),
        name="dkern",
    )(*near(scalars, own_points, *vectors))
    received[0], dkern = lax.optimization_barrier((received[0], dkern))
    if paired:
        received.append(lax.ppermute(received[0], "grp", SWAP))

    message, direction, residual, applied, columns, products, turned = call(
        functools.partial(second_kernel, part_count, paired),
        out_shape=(
            shape((devices, 2, own), F32), row_shape, row_shape, row_shape, shape((cols, 128), F32),
            wide_shape, wide_shape,
        ),
        in_specs=[_smem()] * 2 + _vmem(7 + 2 * part_count),
        out_specs=tuple(_vmem(7)),
        name="second",
    )(
        *place,
        *near(scalars, own_right, kernel_first, slope_first, dkern, wide, norm, *kerns, *received),
    )
    received = lax.all_to_all(message, axes, 0, 0, tiled=True)

    solution, final, gradient = call(
        functools.partial(last_kernel, part_count, paired, float(own * devices)),
        out_shape=(result((cols, own), F32), result((cols, own), F32), result((3,), F32)),
        in_specs=[_smem()] * 2 + _vmem(10),
        out_specs=tuple(_hbm(2) + [_smem()]),
        scratch_shapes=[
            pltpu.VMEM((cols, own), F32),
            pltpu.VMEM((cols, own), F32),
            pltpu.SemaphoreType.DMA((2,)),
        ],
        name="last",
    )(
        *place,
        *near(scalars, own_right, direction, residual, applied, columns, wide, products, turned, received),
    )
    return solution, final, gradient


def solution(mesh):
    whole = P(None, ("blk", "grp"))
    return jax.shard_map(
        functools.partial(local, dict(mesh.shape)),
        mesh=mesh,
        in_specs=(whole, whole, P(), P(), P()),
        out_specs=(whole, whole, P()),
        check_vma=False,
    )
```

time: 49.3 us -> 47.6 us (0.966)
  blocking collectives: 29.8 us -> 21.5 us
  starting transfers between devices: 2.81 us -> 7.39 us
  waiting for transfers between devices: 6.12 us -> 8.09 us
    all_to_all x1, blocking collectives: 20.8 us -> 12.4 us  [local(): lax.all_to_all(message, axes, 0, 0, tiled=True, axis_index_groups=groups)]
    ppermute x0 -> x1, starting transfers between devices: none -> 4.13 us  [local(): lax.ppermute(shard, 'blk', [(at, (at + half) % blocks) for at in range(bl...]
    all_to_all x1, waiting for transfers between devices: 4.7 us -> 6.01 us  [local(): received = [lax.all_to_all(message, axes, 0, 0, tiled=True)]]
    ppermute x1, waiting for transfers between devices: 0.29 us -> 0.94 us  [local(): vectors.append(lax.ppermute(vectors[0], 'grp', SWAP))]
    pallas_call x6 -> x7, Pallas kernels: 7.59 us -> 7.61 us  [the longest x2 2.27 us: local(): call(functools.partial(kern_kernel, part > 0), out_shape=tuple(outs), in_...]
  transfers between devices with their start and end apart: 3 -> 4, of which waited for: 3 -> 3; matrix products, arithmetic and copies ran while one was open for 0% -> 0% of each run, Pallas kernels for 6% -> 6%
where the time goes in v5:
time: 47.6 us; the launch traced here: 47.2 us
  blocking collectives  21.5 us (45%)
  waiting for transfers between devices  8.09 us (17%)
  Pallas kernels  7.61 us (16%)
  starting transfers between devices  7.39 us (16%)
  between operations  2.62 us (6%)
    all_to_all x1, blocking collectives, local(): lax.all_to_all(message, axes, 0, 0, tiled=True, axis_index_groups=groups)  12.4 us
    all_to_all x1, blocking collectives, local(): received = lax.all_to_all(message, axes, 0, 0, tiled=True)  9.02 us
    all_to_all x1, waiting for transfers between devices, local(): received = [lax.all_to_all(message, axes, 0, 0, tiled=True)]  6.01 us
    ppermute x1, starting transfers between devices, local(): lax.ppermute(shard, 'blk', [(at, (at + half) % blocks) for at in range(bl...  4.13 us
    all_to_all x1, starting transfers between devices, local(): received = [lax.all_to_all(message, axes, 0, 0, tiled=True)]  3.05 us
    pallas_call x2, Pallas kernels, local(): call(functools.partial(kern_kernel, part > 0), out_shape=tuple(outs), in_...  2.27 us
    pallas_call x1, Pallas kernels, local(): call(functools.partial(dkern_kernel, part_count), out_shape=(shape((devic...  2.2 us
    pallas_call x1, Pallas kernels, local(): call(functools.partial(last_kernel, part_count, paired, float(own * devic...  1.32 us
  transfers between devices with their start and end apart: 4, of which 3 were waited for; matrix products, arithmetic and copies ran while one was open for 0% of the time, Pallas kernels for 6%

profile of v5, /device:TPU:0, one launch (start us, length us, event | category | flops | bytes accessed | tf_op | source)
XLA Modules:
  0.0 47.2 jit_solution(2278824454502251671)
XLA Ops:
  0.6 0.8 %pack.1 = (bf16[96,128]{1,0:T(8,128)(2,1)S(1)}, bf16[64,128]{1,0:T(8,128)(2,1)S(1)}, f32[16,128]{1,0:T(8,128)S(1)}) custom-call(bf16[64,128]{1,0:T(8,128)(2,1)} %points_hbm.1, f32[16,128]{1,0:T(8,128)} %right_hbm.1), custom_call_target="tpu_custom_call" | custom-call | tf_op jit(solution)/shard_map/pack/pallas_call | solution.py:392
  1.4 4.1 %collective-permute-start = (bf16[96,128]{1,0:T(8,128)(2,1)S(1)}, bf16[96,128]{1,0:T(8,128)(2,1)S(1)}, u32[]{:S(2)}, u32[]{:S(2)}) collective-permute-start(bf16[96,128]{1,0:T(8,128)(2,1)S(1)} %get-tuple-element.26.refs_0_), channel_id=1, source_target_pairs={{0,16},{2,18},{4,20},{6,22},{8,24},{10,26},{12,28},{14,30},{16,0},... | collective-permute-start | bytes 73736 | tf_op jit(solution)/shard_map/ppermute | solution.py:403
  7.5 0.0 collective-permute-done.refs_1_
  7.5 0.1 fan.1
  7.5 12.4 %all_to_all.15.part_ref.refs_0_ = bf16[8,2,96,128]{3,2,1,0:T(8,128)(2,1)S(1)} all-to-all(bf16[8,2,96,128]{3,2,1,0:T(8,128)(2,1)S(1)} %get-tuple-element.30), channel_id=1, replica_groups={{0,2,4,6,8,10,12,14},{1,3,5,7,9,11,13,15},{16,18,20,22,24,26,28,30},{17..., dimensions={0} | all-to-all | bytes 786432 | tf_op jit(solution)/shard_map/all_to_all | solution.py:416
  20.0 0.0 collective-permute-start.1
  20.0 0.8 %kern.2 = (bf16[8,128,256]{2,1,0:T(8,128)(2,1)S(1)}, f32[16,128]{1,0:T(8,128)S(1)}) custom-call(f32[8,128]{1,0:T(8,128)S(1)} %get-tuple-element.27.scalars_ref, bf16[64,128]{1,0:T(8,128)(2,1)S(1)} %get-tuple-element.29.points_ref, bf16[8,2,96,128]{3,2,1,0:T(8,128)(2,1)S(1)} %all_to_all.15.part_ref.refs_0_), custom_call_target="tpu_custom_call" | custom-call | tf_op jit(solution)/shard_map/kern/pallas_call | solution.py:427
  20.8 0.9 %collective-permute-done.1.part_ref.refs_1_ = bf16[8,2,96,128]{3,2,1,0:T(8,128)(2,1)S(1)} collective-permute-done((bf16[8,2,96,128]{3,2,1,0:T(8,128)(2,1)S(1)}, bf16[8,2,96,128]{3,2,1,0:T(8,128)(2,1)S(1)}, u32[]{:S(2)}, u32[]{:S(2)}) %collective-permute-start.1) | collective-permute-done | bytes 393248 | tf_op jit(solution)/shard_map/ppermute | solution.py:417
  21.7 1.5 %kern.3 = (bf16[8,128,256]{2,1,0:T(8,128)(2,1)S(1)}, f32[16,128]{1,0:T(8,128)S(1)}, f32[32,8,128]{2,1,0:T(8,128)}) custom-call(f32[8,128]{1,0:T(8,128)S(1)} %get-tuple-element.27.scalars_ref, bf16[64,128]{1,0:T(8,128)(2,1)S(1)} %get-tuple-element.29.points_ref, bf16[8,2,96,128]{3,2,1,0:T(8,128)(2,1)S(1)} %collective-permute-done.1.part_ref.refs_1_, ...), custom_call_target="tpu_custom_call" | custom-call | tf_op jit(solution)/shard_map/kern/pallas_call | solution.py:427
  23.2 3.0 %all-to-all-start.1 = ((f32[32,8,128]{2,1,0:T(8,128)}), f32[32,8,128]{2,1,0:T(8,128)S(1)}, u32[]{:S(2)}, u32[]{:S(2)}) async-start(f32[32,8,128]{2,1,0:T(8,128)} %get-tuple-element.34), calls=%async_computation.1 | async-start | bytes 262144 | tf_op jit(solution)/shard_map/all_to_all | solution.py:436
  26.3 2.2 %dkern.1 = (bf16[16,128,256]{2,1,0:T(8,128)(2,1)S(1)}, f32[16,128]{1,0:T(8,128)S(1)}, f32[16,2,16,128]{3,2,1,0:T(8,128)S(1)}, f32[16,128]{1,0:T(8,128)S(1)}) custom-call(f32[8,128]{1,0:T(8,128)S(1)} %get-tuple-element.27.scalars_ref, bf16[64,128]{1,0:T(8,128)(2,1)S(1)} %get-tuple-element.29.points_ref, ...), custom_call_target="tpu_custom_call" | custom-call | tf_op jit(solution)/shard_map/dkern/pallas_call | solution.py:438
  28.5 6.0 %all-to-all-done.1.refs_2_ = f32[32,8,128]{2,1,0:T(8,128)S(1)} async-done(((f32[32,8,128]{2,1,0:T(8,128)}), f32[32,8,128]{2,1,0:T(8,128)S(1)}, u32[]{:S(2)}, u32[]{:S(2)}) %all-to-all-start.1) | async-done | bytes 131104 | tf_op jit(solution)/shard_map/all_to_all | solution.py:436
  34.5 0.2 collective-permute-start.2
  34.7 1.1 %collective-permute-done.2.refs_3_ = f32[32,8,128]{2,1,0:T(8,128)S(1)} collective-permute-done((f32[32,8,128]{2,1,0:T(8,128)S(1)}, f32[32,8,128]{2,1,0:T(8,128)S(1)}, u32[]{:S(2)}, u32[]{:S(2)}) %collective-permute-start.2) | collective-permute-done | bytes 131104 | tf_op jit(solution)/shard_map/ppermute | solution.py:449
  35.8 1.0 %second.1 = (f32[32,2,128]{2,1,0:T(2,128)S(1)}, f32[16,128]{1,0:T(8,128)S(1)}, f32[16,128]{1,0:T(8,128)S(1)}, f32[16,128]{1,0:T(8,128)S(1)}, f32[16,128]{1,0:T(8...) custom-call(s32[1]{0:T(128)} %bitcast.block_ref, s32[1]{0:T(128)} %bitcast.1.core_ref, ...), custom_call_target="tpu_custom_call" | custom-call | tf_op jit(solution)/shard_map/second/pallas_call | solution.py:451
  36.8 9.0 %all_to_all.16.received_ref = f32[32,2,128]{2,1,0:T(2,128)S(1)} all-to-all(f32[32,2,128]{2,1,0:T(2,128)S(1)} %get-tuple-element.48), channel_id=1, replica_groups=mesh['blk'=16,'grp'=2] {'blk','grp'}, dimensions={0} | all-to-all | bytes 65536 | tf_op jit(solution)/shard_map/all_to_all | solution.py:464
  45.8 1.3 %last.1 = (f32[16,128]{1,0:T(8,128)}, f32[16,128]{1,0:T(8,128)}, f32[3]{0:T(128)}) custom-call(s32[1]{0:T(128)} %bitcast.block_ref, s32[1]{0:T(128)} %bitcast.1.core_ref, f32[8,128]{1,0:T(8,128)S(1)} %get-tuple-element.27.scalars_ref, f32[16,128]{1,0:T(8,128)S(1)} %get-tuple-element.28.right_ref, f32[16,128]{1,0:T(8,128)S(1)} %get-tuple-element.42.direction_ref, ...), custom_call_target="tpu_custom_call" | custom-call | tf_op jit(solution)/shard_map/last/pallas_call | solution.py:466
Async XLA Ops:
  1.4 6.1 %collective-permute-start = (bf16[96,128]{1,0:T(8,128)(2,1)S(1)}, bf16[96,128]{1,0:T(8,128)(2,1)S(1)}, u32[]{:S(2)}, u32[]{:S(2)}) collective-permute-start(bf16[96,128]{1,0:T(8,128)(2,1)S(1)} %get-tuple-element.26.refs_0_), channel_id=1, source_target_pairs={{0,16},{2,18},{4,20},{6,22},{8,24},{10,26},{12,28},{14,30},{16,0},... | collective-permute-start | bytes 73736 | tf_op jit(solution)/shard_map/ppermute | solution.py:403
  20.0 1.7 %collective-permute-start.1 = (bf16[8,2,96,128]{3,2,1,0:T(8,128)(2,1)S(1)}, bf16[8,2,96,128]{3,2,1,0:T(8,128)(2,1)S(1)}, u32[]{:S(2)}, u32[]{:S(2)}) collective-permute-start(bf16[8,2,96,128]{3,2,1,0:T(8,128)(2,1)S(1)} %all_to_all.15.part_ref.refs_0_), channel_id=1, source_target_pairs={{0,1},{1,0},{2,3},{3,2},{4,5},{5,4},{6,7},{7,6},{8,9},{9,8},{10,11... | collective-permute-start | bytes 1179656 | tf_op jit(solution)/shard_map/ppermute | solution.py:417
  23.2 11.3 %all-to-all-start.1 = ((f32[32,8,128]{2,1,0:T(8,128)}), f32[32,8,128]{2,1,0:T(8,128)S(1)}, u32[]{:S(2)}, u32[]{:S(2)}) async-start(f32[32,8,128]{2,1,0:T(8,128)} %get-tuple-element.34), calls=%async_computation.1 | async-start | bytes 262144 | tf_op jit(solution)/shard_map/all_to_all | solution.py:436
  34.5 1.3 %collective-permute-start.2 = (f32[32,8,128]{2,1,0:T(8,128)S(1)}, f32[32,8,128]{2,1,0:T(8,128)S(1)}, u32[]{:S(2)}, u32[]{:S(2)}) collective-permute-start(f32[32,8,128]{2,1,0:T(8,128)S(1)} %all-to-all-done.1.refs_2_), channel_id=1, source_target_pairs={{0,1},{1,0},{2,3},{3,2},{4,5},{5,4},{6,7},{7,6},{8,9},{9,8},{10,11... | collective-permute-start | bytes 393224 | tf_op jit(solution)/shard_map/ppermute | solution.py:449

commit v6 on v5

--- a/solution.py
+++ b/solution.py
@@ -128,45 +128,38 @@
             message_ref[peer] = total[first : first + rows]
 
 
-def dkern_kernel(part_count, scalars_ref, points_ref, *refs):
-    parts = refs[:part_count]
-    tiles_ref, total_ref, wide_ref, norm_ref = refs[part_count:]
+def dkern_kernel(has_before, scalars_ref, points_ref, part_ref, *refs):
+    before = refs[0][...] if has_before else None
+    tiles_ref, wide_ref, total_ref, norm_ref = refs[1 if has_before else 0 :]
     feats, own = points_ref.shape
     cols = total_ref.shape[0]
     distances = Distances(scalars_ref, points_ref)
     slope = 1.0 / (3.0 * LOG2E * LOG2E * LOG2E * distances.scale)
-    total = jnp.zeros((cols, own), F32)
-    norms = []
-    base = 0
-    for part in parts:
-        steps, sides = part.shape[:2]
-
-        def one_pair(step, carried, part=part, base=base):
-            total, norm = carried
-            norm = list(norm)
-            vectors = []
-            for side in range(sides):
-                reduced, root = distances(part[step, side, 0:feats, :])
-                tile = (reduced * slope) * ((root + LOG2E) * jnp.exp2(-root))
-                tiles_ref[base + step, :, pl.ds(side * own, own)] = tile.astype(BF16)
-                high = part[step, side, feats : feats + cols, :]
-                low = part[step, side, feats + cols : feats + 2 * cols, :]
-                right = high.astype(F32) + low.astype(F32)
-                wide_ref[base + step, side] = right
-                norm[side] = norm[side] + right * right
-                vectors.append(high)
-            vectors = jnp.concatenate(vectors, axis=1)
-            total = total + lax.dot_general(
-                vectors, tiles_ref[base + step], NT, preferred_element_type=F32
-            )
-            return total, tuple(norm)
-
-        zeros = (jnp.zeros((cols, own), F32),) * sides
-        total, norm = lax.fori_loop(0, steps, one_pair, (total, zeros), unroll=unrolled(steps, 4))
-        norms.append(norm)
-        base += steps
+    steps, sides = part_ref.shape[:2]
+    zero = jnp.zeros((cols, own), F32)
+
+    def one_pair(step, carried):
+        total, norm = carried
+        norm = list(norm)
+        vectors = []
+        for side in range(sides):
+            reduced, root = distances(part_ref[step, side, 0:feats, :])
+            tile = (reduced * slope) * ((root + LOG2E) * jnp.exp2(-root))
+            tiles_ref[step, :, pl.ds(side * own, own)] = tile.astype(BF16)
+            high = part_ref[step, side, feats : feats + cols, :]
+            low = part_ref[step, side, feats + cols : feats + 2 * cols, :]
+            right = high.astype(F32) + low.astype(F32)
+            wide_ref[step, side] = right
+            norm[side] = norm[side] + right * right
+            vectors.append(high)
+        vectors = jnp.concatenate(vectors, axis=1)
+        total = total + lax.dot_general(vectors, tiles_ref[step], NT, preferred_element_type=F32)
+        return total, tuple(norm)
+
+    start = (before if has_before else zero, (zero,) * sides)
+    total, norm = lax.fori_loop(0, steps, one_pair, start, unroll=unrolled(steps, 8))
     total_ref[...] = total
-    norm_ref[...] = jnp.broadcast_to(lane_sum(joined(norms)), norm_ref.shape)
+    norm_ref[...] = jnp.broadcast_to(lane_sum(functools.reduce(jnp.add, norm)), norm_ref.shape)
 
 
 def from_lanes(row, first, cols):
@@ -185,21 +178,22 @@
 
 
 def second_kernel(
-    part_count, paired, block_ref, core_ref, scalars_ref, right_ref, kernel_ref, slope_ref, dkern_ref, wide_ref,
-    norm_ref, *refs
+    part_count, paired, block_ref, core_ref, scalars_ref, right_ref, kernel_ref, slope_ref,
+    *refs
 ):
-    kerns = refs[:part_count]
-    received = refs[part_count : 2 * part_count]
+    kerns, dkerns, wides, norms, received, outs = [
+        refs[group * part_count : (group + 1) * part_count] for group in range(5)
+    ] + [refs[5 * part_count :]]
     (
         message_ref, direction_ref, residual_ref, applied_ref, columns_ref, products_ref, turned_ref,
-    ) = refs[2 * part_count :]
+    ) = outs
     cols, own = right_ref.shape
-    sides = wide_ref.shape[1]
+    sides = wides[0].shape[1]
     amplitude = scalars_ref[1:2, :]
     jitter = scalars_ref[2:3, :]
     low_core = core_ref[0] == 0
     zero = jnp.zeros((cols, own), F32)
-    norm = norm_ref[:, 0:1]
+    norm = functools.reduce(jnp.add, [norm_ref[:, 0:1] for norm_ref in norms])
     steps = kerns[0].shape[0]
 
     sums = []
@@ -216,7 +210,7 @@
                         axis=0,
                     )
                 products_ref[part * steps + index, side] = product
-                right = wide_ref[part * steps + index, side]
+                right = wides[part][index, side]
                 applied = amplitude * product + jitter * right
                 carried[0][side] = carried[0][side] + right * applied
                 carried[1][side] = carried[1][side] + applied * applied
@@ -234,30 +228,30 @@
     slopes = zero
     for part in range(part_count):
         def second_pass(index, carried, part=part):
-            total, slopes, norms = carried
-            norms = list(norms)
+            total, slopes, lengths = carried
+            lengths = list(lengths)
             rounded = []
             for side in range(sides):
-                right = wide_ref[part * steps + index, side]
+                right = wides[part][index, side]
                 product = products_ref[part * steps + index, side]
                 residual = right - step * (amplitude * product + jitter * right)
                 direction = residual + turn * right
                 turned_ref[part * steps + index, side] = direction
-                norms[side] = norms[side] + residual * residual
+                lengths[side] = lengths[side] + residual * residual
                 rounded.append(direction)
             rounded = jnp.concatenate(rounded, axis=1).astype(BF16)
             total = total + lax.dot_general(
                 rounded, kerns[part][index], NT, preferred_element_type=F32
             )
             slopes = slopes + lax.dot_general(
-                rounded, dkern_ref[part * steps + index], NT, preferred_element_type=F32
+                rounded, dkerns[part][index], NT, preferred_element_type=F32
             )
-            return total, slopes, tuple(norms)
-
-        total, slopes, norms = lax.fori_loop(
+            return total, slopes, tuple(lengths)
+
+        total, slopes, lengths = lax.fori_loop(
             0, steps, second_pass, (total, slopes, (zero,) * sides), unroll=unrolled(steps, 8)
         )
-        sums.append(norms)
+        sums.append(lengths)
     norm_next = lane_sum(joined(sums))
 
     right = right_ref[...]
@@ -291,12 +285,13 @@
 
 
 def last_kernel(
-    part_count, paired, points_total, block_ref, core_ref, scalars_ref, right_ref, direction_ref, residual_ref,
-    applied_ref, columns_ref, wide_ref, products_ref, turned_ref, received_ref,
-    solution_hbm, final_hbm, gradient_ref, solution_ref, final_ref, sems
+    part_count, paired, points_total, block_ref, core_ref, scalars_ref, right_ref, direction_ref,
+    residual_ref, applied_ref, columns_ref, products_ref, turned_ref, received_ref, *refs
 ):
+    wides = refs[:part_count]
+    solution_hbm, final_hbm, gradient_ref, solution_ref, final_ref, sems = refs[part_count:]
     cols, own = right_ref.shape
-    amplitude = scalars_ref[1:2, :]
+    amplitude = scalars_ref[1:2, 0:1]
     devices = received_ref.shape[0]
 
     def gather_sums(device, carried):
@@ -326,7 +321,7 @@
     turn = columns_ref[:, 3:4]
     dots = turn * norm
     squares = norm_next + turn * dots
-    steps, sides = wide_ref.shape[0] // part_count, wide_ref.shape[1]
+    steps, sides = wides[0].shape[:2]
     zero = jnp.zeros((cols, own), F32)
     row_zero = jnp.zeros((1, own), F32)
     sums = []
@@ -335,7 +330,7 @@
             carried = [list(sums) for sums in carried]
             block = part * steps + index
             for side in range(sides):
-                vector = step * wide_ref[block, side] + step_next * turned_ref[block, side]
+                vector = step * wides[part][index, side] + step_next * turned_ref[block, side]
                 rounded = vector.astype(BF16).astype(F32)
                 source = source_of(block_ref, core_ref, paired, steps, part, index, side)
                 carried[0][side] = carried[0][side] + products_ref[block, side] * rounded
@@ -353,8 +348,8 @@
     weight = jnp.where(is_first, 1.0, -1.0 / (cols - 1))
     for slot, (right_form, direction_form) in enumerate((
         (
-            amplitude[:, 0:1] * (step * right_slope + step_next * right_slope_next),
-            amplitude[:, 0:1] * direction_slope,
+            amplitude * (step * right_slope + step_next * right_slope_next),
+            amplitude * direction_slope,
         ),
         (right_kernel, direction_kernel),
         (step * norm + step_next * dots, (step * dots + step_next * squares)[0:1]),
@@ -418,55 +413,68 @@
     else:
         vectors = [lax.all_to_all(message, axes, 0, 0, tiled=True).reshape(steps, 2, rows, own)]
 
-    kerns = []
-    total = []
-    for part in range(part_count):
-        outs = [shape((steps, own, 2 * own), BF16), row_shape]
+    tile_shape = shape((steps, own, 2 * own), BF16)
+    wide_shape = shape((steps, 2, cols, own), F32)
+
+    def kern_call(part, vector, *before):
+        outs = [tile_shape, row_shape]
         if part + 1 == part_count:
             outs.append(shape((devices, cols // part_count, own), F32))
-        tiles, *total = call(
+        return call(
             functools.partial(kern_kernel, part > 0),
             out_shape=tuple(outs),
-            in_specs=_vmem(4 if part > 0 else 3),
+            in_specs=_vmem(3 + len(before)),
             out_specs=tuple(_vmem(len(outs))),
             name="kern",
-        )(*near(scalars, own_points, vectors[part], *total))
-        kerns.append(tiles)
-    kernel_first, message = total
+        )(*near(scalars, own_points, vector, *before))
+
+    def dkern_call(vector, *before):
+        return call(
+            functools.partial(dkern_kernel, len(before) > 0),
+            out_shape=(tile_shape, wide_shape, row_shape, row_shape),
+            in_specs=_vmem(3 + len(before)),
+            out_specs=tuple(_vmem(4)),
+            name="dkern",
+        )(*near(scalars, own_points, vector, *before))
+
+    kerns = [kern_call(0, vectors[0])]
+    dkerns = []
+    if paired:
+        dkerns.append(dkern_call(vectors[0]))
+        vectors[1], *dkerns[0] = lax.optimization_barrier((vectors[1], *dkerns[0]))
+        kerns.append(kern_call(1, vectors[1], kerns[0][1]))
+    kernel_first, message = kerns[-1][1:]
     received = [lax.all_to_all(message, axes, 0, 0, tiled=True)]
-    wide_shape = shape((devices // 2, 2, cols, own), F32)
-    dkern, slope_first, wide, norm = call(
-        functools.partial(dkern_kernel, part_count),
-        out_shape=(
-            shape((devices // 2, own, 2 * own), BF16), row_shape, wide_shape, row_shape,
-        ),
-        in_specs=_vmem(2 + part_count),
-        out_specs=tuple(_vmem(4)),
-        name="dkern",
-    )(*near(scalars, own_points, *vectors))
-    received[0], dkern = lax.optimization_barrier((received[0], dkern))
     if paired:
+        received[0], vectors[1] = lax.optimization_barrier((received[0], vectors[1]))
         received.append(lax.ppermute(received[0], "grp", SWAP))
-
+        dkerns.append(dkern_call(vectors[1], dkerns[0][2]))
+    else:
+        dkerns.append(dkern_call(vectors[0]))
+    kerns = [tiles for tiles, *rest in kerns]
+    slope_first = dkerns[-1][2]
+    dkerns, wides, norms = [[outs[slot] for outs in dkerns] for slot in (0, 1, 3)]
+
+    both_shape = shape((devices // 2, 2, cols, own), F32)
     message, direction, residual, applied, columns, products, turned = call(
         functools.partial(second_kernel, part_count, paired),
         out_shape=(
             shape((devices, 2, own), F32), row_shape, row_shape, row_shape, shape((cols, 128), F32),
-            wide_shape, wide_shape,
+            both_shape, both_shape,
         ),
-        in_specs=[_smem()] * 2 + _vmem(7 + 2 * part_count),
+        in_specs=[_smem()] * 2 + _vmem(4 + 5 * part_count),
         out_specs=tuple(_vmem(7)),
         name="second",
     )(
         *place,
-        *near(scalars, own_right, kernel_first, slope_first, dkern, wide, norm, *kerns, *received),
+        *near(scalars, own_right, kernel_first, slope_first, *kerns, *dkerns, *wides, *norms, *received),
     )
     received = lax.all_to_all(message, axes, 0, 0, tiled=True)
 
     solution, final, gradient = call(
         functools.partial(last_kernel, part_count, paired, float(own * devices)),
         out_shape=(result((cols, own), F32), result((cols, own), F32), result((3,), F32)),
-        in_specs=[_smem()] * 2 + _vmem(10),
+        in_specs=[_smem()] * 2 + _vmem(9 + part_count),
         out_specs=tuple(_hbm(2) + [_smem()]),
         scratch_shapes=[
             pltpu.VMEM((cols, own), F32),
@@ -476,7 +484,7 @@
         name="last",
     )(
         *place,
-        *near(scalars, own_right, direction, residual, applied, columns, wide, products, turned, received),
+        *near(scalars, own_right, direction, residual, applied, columns, products, turned, received, *wides),
     )
     return solution, final, gradient
 

time: 47.6 us -> 46.8 us (0.983)
  blocking collectives: 21.5 us -> 32.6 us
  waiting for transfers between devices: 8.09 us -> 0.39 us
  starting transfers between devices: 7.39 us -> 4.35 us
  Pallas kernels: 7.61 us -> 6.46 us
    all_to_all x0 -> x1, blocking collectives: none -> 11.1 us  [local(): received = [lax.all_to_all(message, axes, 0, 0, tiled=True)]]
    all_to_all x1 -> x0, waiting for transfers between devices: 6.01 us -> none  [local(): received = [lax.all_to_all(message, axes, 0, 0, tiled=True)]]
    all_to_all x1 -> x0, starting transfers between devices: 3.05 us -> none  [local(): received = [lax.all_to_all(message, axes, 0, 0, tiled=True)]]
    pallas_call x3 -> x4, Pallas kernels: 4.46 us -> 3.3 us  [the longest x2 1.68 us: dkern_call(): call(functools.partial(dkern_kernel, len(before) > 0), out_shape=(tile_sh...]
    ppermute x1, waiting for transfers between devices: 0.94 us -> 0.07 us  [local(): vectors.append(lax.ppermute(vectors[0], 'grp', SWAP))]
    ppermute x1, waiting for transfers between devices: 1.13 us -> 0.32 us  [local(): received.append(lax.ppermute(received[0], 'grp', SWAP))]
  transfers between devices with their start and end apart: 4 -> 3, of which waited for: 3 -> 2; matrix products, arithmetic and copies ran while one was open for 0% -> 0% of each run, Pallas kernels for 6% -> 5%
where the time goes in v6:
time: 46.8 us; the launch traced here: 46.4 us
  blocking collectives  32.6 us (70%)
  Pallas kernels  6.46 us (14%)
  starting transfers between devices  4.35 us (9%)
  between operations  2.62 us (6%)
    all_to_all x1, blocking collectives, local(): lax.all_to_all(message, axes, 0, 0, tiled=True, axis_index_groups=groups)  12.4 us
    all_to_all x1, blocking collectives, local(): received = [lax.all_to_all(message, axes, 0, 0, tiled=True)]  11.1 us
    all_to_all x1, blocking collectives, local(): received = lax.all_to_all(message, axes, 0, 0, tiled=True)  9.02 us
    ppermute x1, starting transfers between devices, local(): lax.ppermute(shard, 'blk', [(at, (at + half) % blocks) for at in range(bl...  4.13 us
    pallas_call x2, Pallas kernels, dkern_call(): call(functools.partial(dkern_kernel, len(before) > 0), out_shape=(tile_sh...  1.68 us
    pallas_call x2, Pallas kernels, kern_call(): call(functools.partial(kern_kernel, part > 0), out_shape=tuple(outs), in_...  1.62 us
    pallas_call x1, Pallas kernels, local(): call(functools.partial(last_kernel, part_count, paired, float(own * devic...  1.32 us
    pallas_call x1, Pallas kernels, local(): call(functools.partial(second_kernel, part_count, paired), out_shape=(sha...  1.01 us
  transfers between devices with their start and end apart: 3, of which 2 were waited for; matrix products, arithmetic and copies ran while one was open for 0% of the time, Pallas kernels for 5%

profile of v6, /device:TPU:0, one launch (start us, length us, event | category | flops | bytes accessed | tf_op | source)
XLA Modules:
  0.0 46.4 jit_solution(7068393695172495560)
XLA Ops:
  0.6 0.8 %pack.1 = (bf16[96,128]{1,0:T(8,128)(2,1)S(1)}, bf16[64,128]{1,0:T(8,128)(2,1)S(1)}, f32[16,128]{1,0:T(8,128)S(1)}) custom-call(bf16[64,128]{1,0:T(8,128)(2,1)} %points_hbm.1, f32[16,128]{1,0:T(8,128)} %right_hbm.1), custom_call_target="tpu_custom_call" | custom-call | tf_op jit(solution)/shard_map/pack/pallas_call | solution.py:387
  1.4 4.1 %collective-permute-start = (bf16[96,128]{1,0:T(8,128)(2,1)S(1)}, bf16[96,128]{1,0:T(8,128)(2,1)S(1)}, u32[]{:S(2)}, u32[]{:S(2)}) collective-permute-start(bf16[96,128]{1,0:T(8,128)(2,1)S(1)} %get-tuple-element.35.refs_0_), channel_id=1, source_target_pairs={{0,16},{2,18},{4,20},{6,22},{8,24},{10,26},{12,28},{14,30},{16,0},... | collective-permute-start | bytes 73736 | tf_op jit(solution)/shard_map/ppermute | solution.py:398
  7.5 0.0 collective-permute-done.refs_1_
  7.5 0.1 fan.1
  7.5 12.4 %all_to_all.15.part_ref = bf16[8,2,96,128]{3,2,1,0:T(8,128)(2,1)S(1)} all-to-all(bf16[8,2,96,128]{3,2,1,0:T(8,128)(2,1)S(1)} %get-tuple-element.39), channel_id=1, replica_groups={{0,2,4,6,8,10,12,14},{1,3,5,7,9,11,13,15},{16,18,20,22,24,26,28,30},{17..., dimensions={0} | all-to-all | bytes 786432 | tf_op jit(solution)/shard_map/all_to_all | solution.py:411
  20.0 0.0 collective-permute-start.1
  20.0 0.8 %kern.2 = (bf16[8,128,256]{2,1,0:T(8,128)(2,1)S(1)}, f32[16,128]{1,0:T(8,128)S(1)}) custom-call(f32[8,128]{1,0:T(8,128)S(1)} %get-tuple-element.36.scalars_ref, bf16[64,128]{1,0:T(8,128)(2,1)S(1)} %get-tuple-element.38.points_ref, bf16[8,2,96,128]{3,2,1,0:T(8,128)(2,1)S(1)} %all_to_all.15.part_ref), custom_call_target="tpu_custom_call" | custom-call | tf_op jit(solution)/shard_map/kern/pallas_call | solution.py:423
  20.8 0.9 %dkern.2 = (bf16[8,128,256]{2,1,0:T(8,128)(2,1)S(1)}, f32[8,2,16,128]{3,2,1,0:T(8,128)S(1)}, f32[16,128]{1,0:T(8,128)S(1)}, f32[16,128]{1,0:T(8,128)S(1)}) custom-call(f32[8,128]{1,0:T(8,128)S(1)} %get-tuple-element.36.scalars_ref, bf16[64,128]{1,0:T(8,128)(2,1)S(1)} %get-tuple-element.38.points_ref, bf16[8,2,96,128]{3,2,1,0:T(8,128)(2,1)S(1)} %all_to_all.15.part_ref), custom_call_target="tpu_custom_call" | custom-call | tf_op jit(solution)/shard_map/dkern/pallas_call | solution.py:432
  21.6 0.1 collective-permute-done.1.part_ref
  21.7 0.8 %kern.3 = (bf16[8,128,256]{2,1,0:T(8,128)(2,1)S(1)}, f32[16,128]{1,0:T(8,128)S(1)}, f32[32,8,128]{2,1,0:T(8,128)S(1)}) custom-call(f32[8,128]{1,0:T(8,128)S(1)} %get-tuple-element.36.scalars_ref, bf16[64,128]{1,0:T(8,128)(2,1)S(1)} %get-tuple-element.38.points_ref, bf16[8,2,96,128]{3,2,1,0:T(8,128)(2,1)S(1)} %collective-permute-done.1.part_ref, ...), custom_call_target="tpu_custom_call" | custom-call | tf_op jit(solution)/shard_map/kern/pallas_call | solution.py:423
  22.6 11.1 %all_to_all.16.refs_8_ = f32[32,8,128]{2,1,0:T(8,128)S(1)} all-to-all(f32[32,8,128]{2,1,0:T(8,128)S(1)} %get-tuple-element.47), channel_id=1, replica_groups=mesh['blk'=16,'grp'=2] {'blk','grp'}, dimensions={0} | all-to-all | bytes 262144 | tf_op jit(solution)/shard_map/all_to_all | solution.py:447
  33.7 0.2 collective-permute-start.2
  33.9 0.8 %dkern.3 = (bf16[8,128,256]{2,1,0:T(8,128)(2,1)S(1)}, f32[8,2,16,128]{3,2,1,0:T(8,128)S(1)}, f32[16,128]{1,0:T(8,128)S(1)}, f32[16,128]{1,0:T(8,128)S(1)}) custom-call(f32[8,128]{1,0:T(8,128)S(1)} %get-tuple-element.36.scalars_ref, bf16[64,128]{1,0:T(8,128)(2,1)S(1)} %get-tuple-element.38.points_ref, ...), custom_call_target="tpu_custom_call" | custom-call | tf_op jit(solution)/shard_map/dkern/pallas_call | solution.py:432
  34.7 0.3 collective-permute-done.2.refs_9_
  35.0 1.0 %second.1 = (f32[32,2,128]{2,1,0:T(2,128)S(1)}, f32[16,128]{1,0:T(8,128)S(1)}, f32[16,128]{1,0:T(8,128)S(1)}, f32[16,128]{1,0:T(8,128)S(1)}, f32[16,128]{1,0:T(8...) custom-call(s32[1]{0:T(128)} %bitcast.block_ref, s32[1]{0:T(128)} %bitcast.1.core_ref, ...), custom_call_target="tpu_custom_call" | custom-call | tf_op jit(solution)/shard_map/second/pallas_call | solution.py:459
  36.1 9.0 %all_to_all.17.received_ref = f32[32,2,128]{2,1,0:T(2,128)S(1)} all-to-all(f32[32,2,128]{2,1,0:T(2,128)S(1)} %get-tuple-element.66), channel_id=1, replica_groups=mesh['blk'=16,'grp'=2] {'blk','grp'}, dimensions={0} | all-to-all | bytes 65536 | tf_op jit(solution)/shard_map/all_to_all | solution.py:472
  45.1 1.3 %last.1 = (f32[16,128]{1,0:T(8,128)}, f32[16,128]{1,0:T(8,128)}, f32[3]{0:T(128)}) custom-call(s32[1]{0:T(128)} %bitcast.block_ref, s32[1]{0:T(128)} %bitcast.1.core_ref, f32[8,128]{1,0:T(8,128)S(1)} %get-tuple-element.36.scalars_ref, f32[16,128]{1,0:T(8,128)S(1)} %get-tuple-element.37.right_ref, f32[16,128]{1,0:T(8,128)S(1)} %get-tuple-element.60.direction_ref, ...), custom_call_target="tpu_custom_call" | custom-call | tf_op jit(solution)/shard_map/last/pallas_call | solution.py:474
Async XLA Ops:
  1.4 6.1 %collective-permute-start = (bf16[96,128]{1,0:T(8,128)(2,1)S(1)}, bf16[96,128]{1,0:T(8,128)(2,1)S(1)}, u32[]{:S(2)}, u32[]{:S(2)}) collective-permute-start(bf16[96,128]{1,0:T(8,128)(2,1)S(1)} %get-tuple-element.35.refs_0_), channel_id=1, source_target_pairs={{0,16},{2,18},{4,20},{6,22},{8,24},{10,26},{12,28},{14,30},{16,0},... | collective-permute-start | bytes 73736 | tf_op jit(solution)/shard_map/ppermute | solution.py:398
  20.0 1.7 %collective-permute-start.1 = (bf16[8,2,96,128]{3,2,1,0:T(8,128)(2,1)S(1)}, bf16[8,2,96,128]{3,2,1,0:T(8,128)(2,1)S(1)}, u32[]{:S(2)}, u32[]{:S(2)}) collective-permute-start(bf16[8,2,96,128]{3,2,1,0:T(8,128)(2,1)S(1)} %all_to_all.15.part_ref), channel_id=1, source_target_pairs={{0,1},{1,0},{2,3},{3,2},{4,5},{5,4},{6,7},{7,6},{8,9},{9,8},{10,11... | collective-permute-start | bytes 1179656 | tf_op jit(solution)/shard_map/ppermute | solution.py:412
  33.7 1.3 %collective-permute-start.2 = (f32[32,8,128]{2,1,0:T(8,128)S(1)}, f32[32,8,128]{2,1,0:T(8,128)S(1)}, u32[]{:S(2)}, u32[]{:S(2)}) collective-permute-start(f32[32,8,128]{2,1,0:T(8,128)S(1)} %all_to_all.16.refs_8_), channel_id=1, source_target_pairs={{0,1},{1,0},{2,3},{3,2},{4,5},{5,4},{6,7},{7,6},{8,9},{9,8},{10,11... | collective-permute-start | bytes 393224 | tf_op jit(solution)/shard_map/ppermute | solution.py:450
